TPU v7x, 256 devices: a whole 4x4x8 slice. The times are simulated.
256 devices in a mesh: section: 2 (over z_hi), gy: 32 (over z_lo, x, core), gz: 4 (over y).
Axes of the slice: x: 4, y: 4, z: 8 (z_hi: 2, z_lo: 4; z = z_hi * 4 + z_lo), core: 2. Of those that a mesh axis runs over, the one named last changes fastest.
Arguments:
- inflow: float32 [2, 64, 2, 64, 512], P(None, None, None, 'gy', 'gz'), may hold values from -6 to 6
- weights: float32 [4, 27, 64, 64], P('section'), may hold values from -0.15625 to 0.15625
- biases: float32 [4, 64], P('section'), may hold values from -3 to 3
- cotangent: float32 [2, 64, 2, 64, 512], P(None, None, None, 'gy', 'gz'), may hold values from -6 to 6
Outputs:
- section_out: float32 [2, 2, 64, 2, 64, 512], P('section', None, None, None, 'gy', 'gz')
- section_grad: float32 [2, 2, 64, 2, 64, 512], P('section', None, None, None, 'gy', 'gz')
- weight_grad: float32 [4, 27, 64, 64], P('section')
- bias_grad: float32 [4, 64], P('section')
All inputs are finite; a program needn't handle non-finite values.
Results may differ from a plain program's by a relative error of at most 0.0001.
Values sent between devices are 32-bit elements; how exact they have to be, the bound alone decides.
A program may use at most 128 MiB of HBM per device.

v0:
```python
import math

import jax
import jax.numpy as jnp
from jax import lax
from jax.sharding import PartitionSpec as P


def extended(block, sides, width):
    for axis, dim in sides:
        count = lax.axis_size(axis)
        forward = [(i, i + 1) for i in range(count - 1)]
        backward = [(target, source) for source, target in forward]
        low = lax.ppermute(
            lax.slice_in_dim(block, block.shape[dim] - width, None, axis=dim), axis, forward
        )
        high = lax.ppermute(lax.slice_in_dim(block, 0, width, axis=dim), axis, backward)
        block = jnp.concatenate([low, block, high], axis=dim)
    return block


def passed_along(block, axis, distance):
    devices = range(lax.axis_size(axis))
    route = [(i - distance, i) for i in devices if i - distance in devices]
    return lax.ppermute(block, axis, route)


def stacked_taps(padded, out_sizes, flipped):
    size_x, size_y, size_z = out_sizes
    pieces = []
    for offset in range(27):
        start_x, start_y, start_z = (offset // 9, offset // 3 % 3, offset % 3)
        if flipped:
            start_x, start_y, start_z = (2 - start_x, 2 - start_y, 2 - start_z)
        pieces.append(
            padded[
                :,
                start_x : start_x + size_x,
                start_y : start_y + size_y,
                start_z : start_z + size_z,
            ]
        )
    return jnp.stack(pieces)


def convolve(weight, padded, out_sizes):
    return jnp.einsum(
        "toc,tcxyz->oxyz",
        weight,
        stacked_taps(padded, out_sizes, False),
        precision=lax.Precision.HIGHEST,
    )


def face_rim(values):
    rimmed = extended(values, (("gy", 2), ("gz", 3)), 1)
    return jnp.pad(rimmed, ((0, 0), (1, 1), (0, 0), (0, 0)))


def slope_rim(values):
    rimmed = extended(values, (("gy", 2), ("gz", 3)), 1)
    return jnp.pad(rimmed, ((0, 0), (1, 1), (0, 0), (0, 0)))


def section_forward(weights, biases, current, extents):
    stored = []
    for layer_index in range(weights.shape[0]):
        padded = face_rim(current)
        pre_act = (
            convolve(weights[layer_index], padded, extents)
            + biases[layer_index][:, None, None, None]
        )
        stored.append((padded, pre_act))
        current = jax.nn.silu(pre_act)
    return (stored, current)


def per_device(inflow, weights, biases, cotangent):
    highest = lax.Precision.HIGHEST
    first_section = lax.axis_index("section") == 0
    micro_count = inflow.shape[0]
    layer_count = weights.shape[0]
    extents = inflow.shape[2:]
    blank = jnp.zeros(inflow.shape[1:], jnp.float32)
    received = blank
    stored_all = []
    produced = []
    for step_index in range(micro_count + 1):
        own_input = inflow[step_index] if step_index < micro_count else blank
        current = jnp.where(first_section, own_input, received)
        stored, current = section_forward(weights, biases, current, extents)
        stored_all.append(stored)
        produced.append(current)
        if step_index < micro_count:
            received = passed_along(current, "section", 1)
    section_out = jnp.stack(
        [
            jnp.where(first_section, produced[micro], produced[micro + 1])
            for micro in range(micro_count)
        ]
    )
    cell_count = (
        micro_count
        * extents[0]
        * extents[1]
        * lax.axis_size("gy")
        * extents[2]
        * lax.axis_size("gz")
    )
    grad_scale = 1.0 / math.sqrt(cell_count)
    weight_grads = [jnp.zeros(weights.shape[1:], jnp.float32) for layer_index in range(layer_count)]
    bias_grads = [jnp.zeros(biases.shape[1:], jnp.float32) for layer_index in range(layer_count)]
    returned = blank
    collected = []
    for step_index in range(micro_count + 1):
        later = micro_count - 1 - step_index
        own_grad = cotangent[later] if later >= 0 else blank
        gradient = jnp.where(first_section, returned, own_grad)
        stored = stored_all[micro_count - step_index]
        for layer_index in reversed(range(layer_count)):
            padded, pre_act = stored[layer_index]
            sigmoid_value = jax.nn.sigmoid(pre_act)
            slope_grad = gradient * sigmoid_value * (1.0 + pre_act * (1.0 - sigmoid_value))
            weight_grads[layer_index] = weight_grads[layer_index] + jnp.einsum(
                "oxyz,tcxyz->toc",
                slope_grad,
                stacked_taps(padded, extents, False),
                precision=highest,
            )
            bias_grads[layer_index] = bias_grads[layer_index] + jnp.sum(slope_grad, axis=(1, 2, 3))
            gradient = jnp.einsum(
                "toc,toxyz->cxyz",
                weights[layer_index],
                stacked_taps(slope_rim(slope_grad), extents, True),
                precision=highest,
            )
        collected.append(gradient)
        if step_index < micro_count:
            returned = passed_along(gradient, "section", -1)
    section_grad = jnp.stack(
        [
            jnp.where(
                first_section, collected[micro_count - micro], collected[micro_count - 1 - micro]
            )
            for micro in range(micro_count)
        ]
    )
    weight_total, bias_total = lax.psum(
        (jnp.stack(weight_grads) * grad_scale, jnp.stack(bias_grads) * grad_scale), ("gy", "gz")
    )
    return (section_out[None], section_grad[None], weight_total, bias_total)


def solution(mesh):
    return jax.shard_map(
        per_device,
        mesh=mesh,
        in_specs=(
            P(None, None, None, "gy", "gz"),
            P("section", None, None, None),
            P("section", None),
            P(None, None, None, "gy", "gz"),
        ),
        out_specs=(
            P("section", None, None, None, "gy", "gz"),
            P("section", None, None, None, "gy", "gz"),
            P("section", None, None, None),
            P("section", None),
        ),
        check_vma=False,
    )
```

profile of v0, /device:TPU:1, one launch (start us, length us, event | category | flops | bytes accessed | tf_op | source)
XLA Modules:
  0.0 1627.5 jit_solution(7726312461387545481)
XLA Ops:
  8.3 4.5 collective-permute-start
  14.7 3.6 collective-permute-done.1
  18.5 3.2 collective-permute-start.2
  25.9 4.1 collective-permute-done.3
  32.4 2.5 fusion.143
  34.9 4.7 collective-permute-start.4
  41.6 3.6 collective-permute-done.5
  45.4 3.2 collective-permute-start.6
  49.9 2.8 collective-permute-done.6
  52.7 4.1 collective-permute-done.7
  59.3 2.5 fusion.20
  61.9 8.8 collective-permute-start.8
  70.7 2.7 collective-permute-done.8
  73.4 5.3 collective-permute-start.9
  80.7 3.6 collective-permute-done.10
  84.5 2.9 collective-permute-start.11
  88.9 2.6 collective-permute-done.11
  91.5 4.1 collective-permute-done.12
  98.0 2.5 fusion.18
  100.7 4.3 collective-permute-start.13
  106.9 3.6 collective-permute-done.14
  113.9 2.8 collective-permute-done.15
  116.8 4.1 collective-permute-done.16
  123.4 2.5 fusion.16
  126.0 8.1 collective-permute-start.17
  134.1 2.7 collective-permute-done.17
  136.8 3.6 collective-permute-start.18
  142.4 3.6 collective-permute-done.19
  149.4 2.8 collective-permute-done.20
  152.3 4.1 collective-permute-done.21
  158.8 2.5 fusion.14
  161.4 4.7 collective-permute-start.22
  168.0 3.6 collective-permute-done.23
  177.9 4.1 collective-permute-done.25
  187.2 3.6 collective-permute-start.26
  192.8 3.6 collective-permute-done.27
  199.8 2.8 collective-permute-done.28
  202.6 4.1 collective-permute-done.29
  211.6 4.1 collective-permute-start.30
  217.7 3.6 collective-permute-done.31
  224.7 2.8 collective-permute-done.32
  227.5 4.1 collective-permute-done.33
  237.6 9.2 collective-permute-done.34
  247.0 4.7 collective-permute-start.35
  253.7 3.6 collective-permute-done.36
  261.1 3.0 convolution_bitcast_fusion.2
  264.1 3.8 collective-permute-done.38
  272.7 3.0 collective-permute-start.39
  278.6 2.7 collective-permute-done.40
  284.7 3.0 convolution_bitcast_fusion.3
  287.7 3.9 collective-permute-done.42
  297.8 3.0 fusion.24
  300.8 5.9 collective-permute-done.43
  306.9 3.0 convolution_bitcast_fusion
  310.0 4.3 collective-permute-start.44
  316.2 3.0 fusion.27
  323.5 2.6 collective-permute-done.46
  326.1 4.1 collective-permute-done.47
  335.0 3.0 fusion.23
  339.6 3.9 collective-permute-start.48
  345.4 3.6 collective-permute-done.49
  352.4 324.2 %psum.15 = f32[2,64]{1,0:T(2,128)} all-reduce(f32[2,64]{1,0:T(2,128)S(1)} %maximum_multiply_fusion.1), channel_id=1, replica_groups=mesh['section'=2,'gy'=32,'gz'=4] {'gy','gz'}, use_global_device_ids=true, to_apply=%region_7.8 | all-reduce | flops 128 | bytes 1024 | tf_op jit(solution)/shard_map/psum | solution.py:148
  682.3 935.3 %all-reduce.14.cloned.1.call-done = f32[2,27,64,64]{2,3,1,0:T(8,128)} async-done(((f32[2,27,64,64]{2,3,1,0:T(8,128)}), f32[2,27,64,64]{2,3,1,0:T(8,128)}) %all-reduce.14.cloned.1.call-update) | async-done | bytes 884752 | tf_op jit(solution)/shard_map/psum | solution.py:148
  1617.6 2.7 copy.58
  (466 shorter events, 116.3 us)
Async XLA Ops:
  7.2 1610.4 %all-reduce.14.cloned.1.call-start = ((), (), s32[]{:S(2)}) async-start(), calls=%async_computation | async-start | bytes 3538944 | tf_op jit(solution)/shard_map/psum | solution.py:148
  8.3 6.5 collective-permute-start
  12.8 5.6 collective-permute-start.1
  18.5 7.4 collective-permute-start.2
  21.7 8.2 collective-permute-start.3
  30.9 1.5 copy-start
  34.9 6.6 collective-permute-start.4
  39.6 5.6 collective-permute-start.5
  45.4 7.3 collective-permute-start.6
  48.6 8.2 collective-permute-start.7
  61.9 11.5 collective-permute-start.8
  73.4 7.2 collective-permute-start.9
  78.7 5.6 collective-permute-start.10
  84.5 7.0 collective-permute-start.11
  87.4 8.2 collective-permute-start.12
  100.7 6.2 collective-permute-start.13
  105.0 5.6 collective-permute-start.14
  110.7 6.1 collective-permute-start.15
  112.6 8.2 collective-permute-start.16
  126.0 10.8 collective-permute-start.17
  136.8 5.5 collective-permute-start.18
  140.4 5.6 collective-permute-start.19
  146.2 6.1 collective-permute-start.20
  148.1 8.2 collective-permute-start.21
  158.6 16.9 %copy-start.1 = (f32[2,64,2,2,128]{4,3,2,1,0:T(2,128)S(1)}, f32[2,64,2,2,128]{4,3,2,1,0:T(2,128)}, u32[]{:S(2)}) copy-start(f32[2,64,2,2,128]{4,3,2,1,0:T(2,128)} %param.7) | copy-start | bytes 786436
  161.4 6.6 collective-permute-start.22
  166.1 5.6 collective-permute-start.23
  171.8 6.1 collective-permute-start.24
  173.7 8.2 collective-permute-start.25
  187.2 5.5 collective-permute-start.26
  190.8 5.6 collective-permute-start.27
  196.6 6.1 collective-permute-start.28
  198.5 8.2 collective-permute-start.29
  211.6 6.1 collective-permute-start.30
  215.7 5.6 collective-permute-start.31
  221.5 6.1 collective-permute-start.32
  223.4 8.2 collective-permute-start.33
  236.3 10.5 collective-permute-start.34
  247.0 6.7 collective-permute-start.35
  251.8 5.6 collective-permute-start.36
  257.5 6.5 collective-permute-start.37
  259.6 8.2 collective-permute-start.38
  272.7 5.9 collective-permute-start.39
  275.7 5.6 collective-permute-start.40
  281.5 6.2 collective-permute-start.41
  283.4 8.2 collective-permute-start.42
  296.3 10.4 collective-permute-start.43
  310.0 9.3 collective-permute-start.44
  314.3 5.6 collective-permute-start.45
  320.1 6.1 collective-permute-start.46
  322.0 8.2 collective-permute-start.47
  339.6 5.8 collective-permute-start.48
  343.4 5.6 collective-permute-start.49
  349.2 327.5 %collective-permute-start.50 = (f32[64,2,4,1]{3,0,2,1:T(8,128)S(1)}, f32[64,2,4,1]{3,0,2,1:T(8,128)S(1)}, u32[]{:S(2)}, u32[]{:S(2)}) collective-permute-start(f32[64,2,4,1]{3,0,2,1:T(8,128)S(1)} %get-tuple-element.22), channel_id=1, source_target_pairs={{0,1},{1,2},{2,3},{4,5},{5,6},{6,7},{8,9},{9,10},{10,11},{12,13},{... | collective-permute-start | bytes 6152 | tf_op jit(solution)/shard_map/ppermute | solution.py:14
  351.1 325.6 %collective-permute-start.51 = (f32[64,2,4,1]{3,0,2,1:T(8,128)S(1)}, f32[64,2,4,1]{3,0,2,1:T(8,128)S(1)}, u32[]{:S(2)}, u32[]{:S(2)}) collective-permute-start(f32[64,2,4,1]{3,0,2,1:T(8,128)S(1)} %get-tuple-element.23), channel_id=1, source_target_pairs={{1,0},{2,1},{3,2},{5,4},{6,5},{7,6},{9,8},{10,9},{11,10},{13,12},{... | collective-permute-start | bytes 6152 | tf_op jit(solution)/shard_map/ppermute | solution.py:17
Sparse Core Ops, SparseCore 0:
  339.7 1277.8 all-reduce.13
where the time goes:
time: 1640 us; the launch traced here: 1630 us
  waiting for transfers between devices  1060 us (65%)
  blocking collectives  324 us (20%)
  starting transfers between devices  137 us (8%)
  matrix products  46.1 us (3%)
  local copies, waits for them, and re-layouts  22.3 us (1%)
  between operations  18 us (1%)
    psum x1, waiting for transfers between devices, per_device(): lax.psum((jnp.stack(weight_grads) * grad_scale, jnp.stack(bias_grads) * g...  935 us
    psum x1, blocking collectives, per_device(): lax.psum((jnp.stack(weight_grads) * grad_scale, jnp.stack(bias_grads) * g...  324 us
    ppermute x24, waiting for transfers between devices, extended(): lax.ppermute(lax.slice_in_dim(block, 0, width, axis=dim), axis, backward)  84.5 us
    ppermute x24, starting transfers between devices, extended(): lax.ppermute(lax.slice_in_dim(block, block.shape[dim] - width, None, axis...  77.4 us
    ppermute x24, starting transfers between devices, extended(): lax.ppermute(lax.slice_in_dim(block, 0, width, axis=dim), axis, backward)  39.7 us
  transfers between devices with their start and end apart: 53, of which 37 were waited for; matrix products, arithmetic and copies ran while one was open for 1% of the time, Pallas kernels for 0%

commit v1 on v0

v1 whole, which is shorter than its diff:
```python
import math

import jax
import jax.numpy as jnp
from jax import lax
from jax.experimental import pallas as pl
from jax.experimental.pallas import tpu as pltpu
from jax.sharding import PartitionSpec as P

MESH = pl.DeviceIdType.MESH
F32 = jnp.float32
BF16 = jnp.bfloat16
LAYERS = 4
TAPS = 9
DIRS = [(dy, dz) for dy in (-1, 0, 1) for dz in (-1, 0, 1) if (dy, dz) != (0, 0)]
TAP_ROWS = 96
PACK = 880
CHUNKS = 5
CHUNK = PACK // 2 // CHUNKS
GRAD = 1024


def split_parts(value):
    high = value.astype(BF16)
    return high, (value - high.astype(F32)).astype(BF16)


def source_window(dy, dz):
    rows = {1: pl.ds(2, 1), -1: pl.ds(1, 1), 0: pl.ds(1, 2)}[dy]
    cells = {1: pl.ds(128, 8), -1: pl.ds(8, 8), 0: pl.ds(8, 128)}[dz]
    return rows, cells


def target_window(dy, dz):
    rows = {1: pl.ds(0, 1), -1: pl.ds(3, 1), 0: pl.ds(1, 2)}[dy]
    cells = {1: pl.ds(0, 8), -1: pl.ds(136, 8), 0: pl.ds(8, 128)}[dz]
    return rows, cells


def landed(ref, sem):
    pltpu.make_async_copy(ref, ref, sem).wait()


def kernel(
    scale,
    inflow,
    weights,
    biases,
    cotangent,
    out_act,
    out_grad,
    out_weight,
    out_bias,
    ext,
    patch,
    slope_patch,
    wide_f,
    wide_b,
    packed,
    pre,
    flow,
    stage,
    part,
    final,
    half_in,
    half_sum,
    one_in,
    one_sum,
    two_in,
    two_sum,
    three_in,
    halo_send,
    halo_recv,
    source_send,
    relay_send,
    relay_recv,
    mate_send,
    mate_recv,
    out_send,
    out_recv,
    pair_send,
    pair_recv,
    group_send,
    group_recv,
    deep_send,
    deep_recv,
):
    sec = lax.axis_index("section")
    gy = lax.axis_index("gy")
    gz = lax.axis_index("gz")
    core = gy % 2
    px = (gy // 2) % 4
    zlo = gy // 8
    depth = sec * 4 + zlo
    other = 1 - sec

    def at_depth(level, parity):
        return (level // 4, (level % 4) * 8 + px * 2 + parity, gz)

    def in_plane(first, index):
        on_x = (1 - core) if first else core
        new_gy = gy + on_x * 2 * (index - px)
        new_gz = gz + (1 - on_x) * (index - gz)
        return (sec, new_gy, new_gz)

    mate = (sec, gy + 1 - 2 * core, gz)
    step_sign = 1 - 2 * core
    following = at_depth((depth + step_sign + 8) % 8, core)
    at_end = zlo == 3 * (1 - core)

    def exists(dy, dz):
        ok = None
        for index, delta, count in ((gy, dy, 32), (gz, dz, 4)):
            if delta == 0:
                continue
            good = index > 0 if delta < 0 else index < count - 1
            ok = good if ok is None else jnp.logical_and(ok, good)
        return ok

    lane = lax.broadcasted_iota(jnp.int32, (1, 128), 1)
    left = lane < 64

    def turned(value):
        return pltpu.roll(value, 64, 1)

    for i in range(2):
        for b in range(3):
            for c in range(3):
                tap = b * 3 + c
                base = tap * TAP_ROWS
                middle = weights[i, 9 + tap]
                far = weights[i, 18 + tap]
                near = weights[i, tap]
                packed[2 * sec + i, base : base + 64, :] = jnp.concatenate([middle, far], axis=1)
                packed[2 * sec + i, base + 64 : base + 96, :] = jnp.concatenate(
                    [near[0:32], near[32:64]], axis=1
                )
        row = biases[i : i + 1, :]
        packed[2 * sec + i, 864:880, :] = jnp.broadcast_to(
            jnp.concatenate([row, row], axis=1), (16, 128)
        )

    def clear(rows, cells):
        shape = (8, rows.size, cells.size, 128)
        ext[:, rows, cells, :] = jnp.zeros(shape, F32)

    @pl.when(gy == 0)
    def _():
        clear(pl.ds(0, 1), pl.ds(0, 144))

    @pl.when(gy == 31)
    def _():
        clear(pl.ds(3, 1), pl.ds(0, 144))

    @pl.when(gz == 0)
    def _():
        clear(pl.ds(0, 4), pl.ds(0, 8))

    @pl.when(gz == 3)
    def _():
        clear(pl.ds(0, 4), pl.ds(136, 8))

    def turned_in(ref, y):
        rows = [ref[sec, pl.ds(2 * x + y, 64, stride=4), :] for x in range(2)]
        return jnp.concatenate(rows, axis=0).T

    for y in range(2):
        ext[0, 1 + y, 8:136, :] = turned_in(inflow, y)
        flow[y * 128 : (y + 1) * 128, :] = turned_in(cotangent, y)
    for layer in range(LAYERS):
        part[layer, 864:GRAD, :] = jnp.zeros((GRAD - 864, 128), F32)

    barrier = pltpu.get_barrier_semaphore()

    def greet(device):
        pl.semaphore_signal(barrier, inc=1, device_id=device, device_id_type=MESH)

    for d in range(1, 8):
        greet(at_depth((depth + d) % 8, core))
    for d in range(1, 4):
        greet((sec, gy + 2 * ((px + d) % 4 - px), gz))
        greet((sec, gy, (gz + d) % 4))
    for dy, dz in DIRS:
        if dy != 0:

            @pl.when(exists(dy, dz))
            def _():
                greet((sec, gy + dy, gz + dz))

    sides_y = 2 - jnp.where(gy == 0, 1, 0) - jnp.where(gy == 31, 1, 0)
    sides_z = 2 - jnp.where(gz == 0, 1, 0) - jnp.where(gz == 3, 1, 0)
    pl.semaphore_wait(barrier, 13 + sides_y * (1 + sides_z))

    def send_rims(slot):
        for d, (dy, dz) in enumerate(DIRS):
            rows, cells = source_window(dy, dz)
            rows_to, cells_to = target_window(dy, dz)

            @pl.when(exists(dy, dz))
            def _():
                pltpu.make_async_remote_copy(
                    src_ref=ext.at[slot, rows, cells, :],
                    dst_ref=ext.at[slot, rows_to, cells_to, :],
                    send_sem=halo_send.at[slot, d],
                    recv_sem=halo_recv.at[slot, d],
                    device_id=(sec, gy + dy, gz + dz),
                    device_id_type=MESH,
                ).start()

    def await_rims(slot):
        for d, (dy, dz) in enumerate(DIRS):
            rows_to, cells_to = target_window(dy, dz)

            @pl.when(exists(-dy, -dz))
            def _():
                landed(ext.at[slot, rows_to, cells_to, :], halo_recv.at[slot, d])

    send_rims(0)

    def chunk_of(layer, parity, chunk):
        start = parity * (PACK // 2) + chunk * CHUNK
        return packed.at[layer, pl.ds(pl.multiple_of(start, 8), CHUNK), :]

    @pl.when(at_end)
    def _():
        for i in range(2):
            for chunk in range(CHUNKS):
                piece = chunk_of(2 * sec + i, core, chunk)
                pltpu.make_async_remote_copy(
                    src_ref=piece,
                    dst_ref=piece,
                    send_sem=source_send.at[i, chunk],
                    recv_sem=relay_recv.at[i, chunk],
                    device_id=following,
                    device_id_type=MESH,
                ).start()

    def widen(layer):
        for tap in range(TAPS):
            base = tap * TAP_ROWS
            top = packed[layer, base : base + 64, :]
            near = packed[layer, base + 64 : base + 96, :]
            bottom = jnp.where(
                left, jnp.concatenate([near, turned(near)], axis=0), turned(top)
            )
            high, low = split_parts(jnp.concatenate([top, bottom], axis=0))
            cols = slice(tap * 128, tap * 128 + 128)
            wide_f[layer, 0:128, cols] = high
            wide_f[layer, 128:256, cols] = low
            rows = slice((8 - tap) * 128, (8 - tap) * 128 + 128)
            wide_b[layer, rows, 0:128] = high
            wide_b[layer, rows, 128:256] = low

    def widen_own(i, carry):
        widen(2 * sec + i)
        return carry

    lax.fori_loop(0, 2, widen_own, 0)

    for i in range(2):
        for chunk in range(CHUNKS):
            piece = chunk_of(2 * other + i, core, chunk)
            landed(piece, relay_recv.at[i, chunk])

            @pl.when(jnp.logical_not(at_end))
            def _():
                pltpu.make_async_remote_copy(
                    src_ref=piece,
                    dst_ref=piece,
                    send_sem=relay_send.at[i, chunk],
                    recv_sem=relay_recv.at[i, chunk],
                    device_id=following,
                    device_id_type=MESH,
                ).start()

            pltpu.make_async_remote_copy(
                src_ref=piece,
                dst_ref=piece,
                send_sem=mate_send.at[i, chunk],
                recv_sem=mate_recv.at[i, chunk],
                device_id=mate,
                device_id_type=MESH,
            ).start()
    for i in range(2):
        for chunk in range(CHUNKS):
            landed(chunk_of(2 * other + i, 1 - core, chunk), mate_recv.at[i, chunk])

    def widen_other(i, carry):
        widen(2 * other + i)
        return carry

    lax.fori_loop(0, 2, widen_other, 0)

    def fill(slot, store):
        for c in range(3):
            for row in range(4):
                high, low = split_parts(ext[slot, row, 7 + c : 135 + c, :])
                for y in range(2):
                    b = row - y
                    if 0 <= b <= 2:
                        tap = b * 3 + c
                        store(y, tap, high, low)

    def hand_out(value, keeper, kind, result):
        def put(ref, lead):
            for y in range(2):
                block = value[y * 128 : (y + 1) * 128, :].T
                for x in range(2):
                    where = pl.ds(2 * x + y, 64, stride=4)
                    ref[lead, where, :] = block[x * 64 : (x + 1) * 64, :]

        @pl.when(sec == keeper)
        def _():
            put(result, sec)

        @pl.when(sec != keeper)
        def _():
            put(stage, kind)
            pltpu.make_async_remote_copy(
                src_ref=stage.at[kind],
                dst_ref=result.at[sec],
                send_sem=out_send.at[kind],
                recv_sem=out_recv.at[kind],
                device_id=(other, gy, gz),
                device_id_type=MESH,
            ).start()

    def joined(product):
        return (
            product[0:256, 0:128]
            + product[0:256, 128:256]
            + product[256:512, 0:128]
            + product[256:512, 128:256]
        )

    def forward(layer, carry):
        await_rims(layer)

        def store(y, tap, high, low):
            cols = slice(tap * 128, tap * 128 + 128)
            patch[layer, y * 128 : y * 128 + 128, cols] = high
            patch[layer, 256 + y * 128 : 384 + y * 128, cols] = low

        fill(layer, store)
        product = lax.dot_general(
            patch[layer],
            wide_f[layer],
            (((1,), (1,)), ((), ())),
            preferred_element_type=F32,
        )
        value = joined(product) + packed[layer, 864:865, :]
        pre[layer] = value
        active = value * (1.0 / (1.0 + jnp.exp(-value)))

        @pl.when(layer < LAYERS - 1)
        def _():
            for y in range(2):
                ext[layer + 1, 1 + y, 8:136, :] = active[y * 128 : (y + 1) * 128, :]
            send_rims(layer + 1)

        @pl.when(layer == 1)
        def _():
            hand_out(active, 0, 0, out_act)

        @pl.when(layer == 3)
        def _():
            hand_out(active, 1, 0, out_act)

        return carry

    lax.fori_loop(0, LAYERS, forward, 0)

    index_one = px + core * (gz - px)
    index_two = gz + core * (px - gz)
    offset_half = core * 512
    offset_one = offset_half + index_one * 128
    offset_two = offset_one + index_two * 32
    offset_three = offset_two + zlo * 8

    def rows_at(ref, layer, start, size):
        return ref.at[layer, pl.ds(pl.multiple_of(start, 8), size), :]

    def push(source, target, send, recv, device):
        pltpu.make_async_remote_copy(
            src_ref=source,
            dst_ref=target,
            send_sem=send,
            recv_sem=recv,
            device_id=device,
            device_id_type=MESH,
        ).start()

    def reduce_start(layer):
        push(
            rows_at(part, layer, (1 - core) * 512, 512),
            half_in.at[layer],
            pair_send.at[0, layer],
            pair_recv.at[0, layer],
            mate,
        )

    def reduce_half(layer):
        landed(half_in.at[layer], pair_recv.at[0, layer])
        half_sum[layer] = (
            part[layer, pl.ds(pl.multiple_of(offset_half, 8), 512), :] + half_in[layer]
        )
        for d in range(1, 4):
            peer = (index_one + d) % 4
            push(
                rows_at(half_sum, layer, peer * 128, 128),
                one_in.at[layer, 3 - d],
                group_send.at[0, layer, 3 - d],
                group_recv.at[0, layer, 3 - d],
                in_plane(True, peer),
            )

    def reduce_one(layer):
        for s in range(3):
            landed(one_in.at[layer, s], group_recv.at[0, layer, s])
        own = half_sum[layer, pl.ds(pl.multiple_of(index_one * 128, 8), 128), :]
        one_sum[layer] = (own + one_in[layer, 0]) + (one_in[layer, 1] + one_in[layer, 2])
        for d in range(1, 4):
            peer = (index_two + d) % 4
            push(
                rows_at(one_sum, layer, peer * 32, 32),
                two_in.at[layer, 3 - d],
                group_send.at[1, layer, 3 - d],
                group_recv.at[1, layer, 3 - d],
                in_plane(False, peer),
            )

    def reduce_two(layer):
        for s in range(3):
            landed(two_in.at[layer, s], group_recv.at[1, layer, s])
        own = one_sum[layer, pl.ds(pl.multiple_of(index_two * 32, 8), 32), :]
        two_sum[layer] = (own + two_in[layer, 0]) + (two_in[layer, 1] + two_in[layer, 2])
        for d in range(1, 8):
            peer = (depth + d) % 8

            @pl.when(peer // 4 == layer // 2)
            def _():
                push(
                    rows_at(two_sum, layer, (peer % 4) * 8, 8),
                    three_in.at[layer, 7 - d],
                    deep_send.at[layer, 7 - d],
                    deep_recv.at[layer, 7 - d],
                    at_depth(peer, core),
                )

    def gather_three(layer):
        for s in range(7):
            landed(three_in.at[layer, s], deep_recv.at[layer, s])
        total = two_sum[layer, pl.ds(pl.multiple_of(zlo * 8, 8), 8), :]
        for s in range(7):
            total = total + three_in[layer, s]
        start = pl.multiple_of(offset_three, 8)
        final[layer, pl.ds(start, 8), :] = total * scale
        for d in range(1, 4):
            piece = rows_at(final, layer, offset_three, 8)
            push(
                piece,
                piece,
                group_send.at[2, layer, 3 - d],
                group_recv.at[2, layer, 3 - d],
                at_depth(sec * 4 + (zlo + d) % 4, core),
            )

    def gathered(layer, stage_at, base, index, size):
        for s in range(3):
            sender = (index + 1 + s) % 4
            piece = rows_at(final, layer, base + sender * size, size)
            landed(piece, group_recv.at[stage_at, layer, s])

    def gather_two(layer):
        gathered(layer, 2, offset_two, zlo, 8)
        for d in range(1, 4):
            piece = rows_at(final, layer, offset_two, 32)
            push(
                piece,
                piece,
                group_send.at[3, layer, 3 - d],
                group_recv.at[3, layer, 3 - d],
                in_plane(False, (index_two + d) % 4),
            )

    def gather_one(layer):
        gathered(layer, 3, offset_one, index_two, 32)
        for d in range(1, 4):
            piece = rows_at(final, layer, offset_one, 128)
            push(
                piece,
                piece,
                group_send.at[4, layer, 3 - d],
                group_recv.at[4, layer, 3 - d],
                in_plane(True, (index_one + d) % 4),
            )

    def gather_half(layer):
        gathered(layer, 4, offset_half, index_one, 128)
        piece = rows_at(final, layer, offset_half, 512)
        push(piece, piece, pair_send.at[1, layer], pair_recv.at[1, layer], mate)

    def unpack(layer):
        i = layer % 2
        landed(rows_at(final, layer, (1 - core) * 512, 512), pair_recv.at[1, layer])
        for tap in range(TAPS):
            base = tap * TAP_ROWS
            top = final[layer, base : base + 64, :]
            near = final[layer, base + 64 : base + 96, :]
            out_weight[i, 9 + tap] = top[:, 0:64]
            out_weight[i, 18 + tap] = turned(top)[:, 0:64]
            out_weight[i, tap, 0:32, :] = near[:, 0:64]
            out_weight[i, tap, 32:64, :] = turned(near)[:, 0:64]
        out_bias[i : i + 1, :] = final[layer, 864:865, 0:64]

    everywhere = [reduce_half, reduce_one, reduce_two]
    at_home = [gather_three, gather_two, gather_one, gather_half, unpack]

    def backward(step, carry):
        layer = LAYERS - 1 - step
        slot = LAYERS + layer
        value = pre[layer]
        sigma = 1.0 / (1.0 + jnp.exp(-value))
        slope = flow[...] * sigma * (1.0 + value * (1.0 - sigma))
        for y in range(2):
            ext[slot, 1 + y, 8:136, :] = slope[y * 128 : (y + 1) * 128, :]
        send_rims(slot)

        across = jnp.concatenate([slope[0:128, :].T, slope[128:256, :].T], axis=1)
        high, low = split_parts(across)
        sides = jnp.concatenate(
            [
                jnp.concatenate([high, high], axis=1),
                jnp.concatenate([low, low], axis=1),
            ],
            axis=0,
        )
        product = jnp.dot(sides, patch[layer], preferred_element_type=F32)
        for tap in range(TAPS):
            cols = slice(tap * 128, tap * 128 + 128)
            block = product[0:128, cols] + product[128:256, cols]
            base = tap * TAP_ROWS
            flipped = turned(block[64:128, :])
            part[layer, base : base + 64, :] = block[0:64, :] + jnp.where(left, flipped, 0.0)
            part[layer, base + 64 : base + 96, :] = jnp.where(
                left, block[64:96, :], flipped[32:64, :]
            )
        sums = jnp.sum(slope, axis=0, keepdims=True)
        part[layer, 864:865, :] = sums + turned(sums)
        reduce_start(layer)
        for k, tick in enumerate(everywhere):

            @pl.when(layer + k + 1 < LAYERS)
            def _():
                tick(layer + k + 1)

        await_rims(slot)

        def store(y, tap, high, low):
            cols = slice(tap * 128, tap * 128 + 128)
            slope_patch[y * 128 : y * 128 + 128, cols] = high
            slope_patch[256 + y * 128 : 384 + y * 128, cols] = low

        fill(slot, store)
        gradient = joined(
            jnp.dot(slope_patch[...], wide_b[layer], preferred_element_type=F32)
        )
        flow[...] = gradient

        @pl.when(layer == 2)
        def _():
            hand_out(gradient, 1, 1, out_grad)

        @pl.when(layer == 0)
        def _():
            hand_out(gradient, 0, 1, out_grad)

        return carry

    lax.fori_loop(0, LAYERS, backward, 0)

    for round_at in range(8):
        for layer in reversed(range(LAYERS)):
            tick = layer + round_at
            if tick < 3:
                everywhere[tick](layer)
            elif tick < 8:

                @pl.when(sec == layer // 2)
                def _():
                    at_home[tick - 3](layer)

    landed(out_act.at[1 - sec], out_recv.at[0])
    landed(out_grad.at[1 - sec], out_recv.at[1])

    def drain_rims(slot, carry):
        for d, (dy, dz) in enumerate(DIRS):
            rows, cells = source_window(dy, dz)

            @pl.when(exists(dy, dz))
            def _():
                landed(ext.at[slot, rows, cells, :], halo_send.at[slot, d])

        return carry

    lax.fori_loop(0, 8, drain_rims, 0)
    for i in range(2):
        for chunk in range(CHUNKS):

            @pl.when(at_end)
            def _():
                landed(chunk_of(2 * sec + i, core, chunk), source_send.at[i, chunk])

            @pl.when(jnp.logical_not(at_end))
            def _():
                landed(chunk_of(2 * other + i, core, chunk), relay_send.at[i, chunk])

            landed(chunk_of(2 * other + i, core, chunk), mate_send.at[i, chunk])
    for kind in range(2):
        landed(stage.at[kind], out_send.at[kind])

    def drain_sums(layer, carry):
        home = sec == layer // 2
        landed(half_in.at[layer], pair_send.at[0, layer])
        for s in range(3):
            landed(one_in.at[layer, s], group_send.at[0, layer, s])
            landed(two_in.at[layer, s], group_send.at[1, layer, s])
        for d in range(1, 8):

            @pl.when(((depth + d) % 8) // 4 == layer // 2)
            def _():
                landed(three_in.at[layer, 7 - d], deep_send.at[layer, 7 - d])

        @pl.when(home)
        def _():
            for s in range(3):
                landed(three_in.at[layer, s], group_send.at[2, layer, s])
                landed(two_in.at[layer, s], group_send.at[3, layer, s])
                landed(one_in.at[layer, s], group_send.at[4, layer, s])
            landed(half_in.at[layer], pair_send.at[1, layer])

        return carry

    lax.fori_loop(0, LAYERS, drain_sums, 0)


def per_device(inflow, weights, biases, cotangent):
    micro, channels, nx, ny, nz = inflow.shape
    cells = micro * nx * ny * lax.axis_size("gy") * nz * lax.axis_size("gz")
    scale = 1.0 / math.sqrt(cells)
    rows = channels * nx * ny
    vmem = pltpu.VMEM
    dma = pltpu.SemaphoreType.DMA
    scratch = [
        vmem((8, 4, 144, 128), F32),
        vmem((LAYERS, 512, TAPS * 128), BF16),
        vmem((512, TAPS * 128), BF16),
        vmem((LAYERS, 256, TAPS * 128), BF16),
        vmem((LAYERS, TAPS * 128, 256), BF16),
        vmem((LAYERS, PACK, 128), F32),
        vmem((LAYERS, 256, 128), F32),
        vmem((256, 128), F32),
        vmem((2, 256, 128), F32),
        vmem((LAYERS, GRAD, 128), F32),
        vmem((LAYERS, GRAD, 128), F32),
        vmem((LAYERS, 512, 128), F32),
        vmem((LAYERS, 512, 128), F32),
        vmem((LAYERS, 3, 128, 128), F32),
        vmem((LAYERS, 128, 128), F32),
        vmem((LAYERS, 3, 32, 128), F32),
        vmem((LAYERS, 32, 128), F32),
        vmem((LAYERS, 7, 8, 128), F32),
        dma((8, 8)),
        dma((8, 8)),
        dma((2, CHUNKS)),
        dma((2, CHUNKS)),
        dma((2, CHUNKS)),
        dma((2, CHUNKS)),
        dma((2, CHUNKS)),
        dma((2,)),
        dma((2,)),
        dma((2, LAYERS)),
        dma((2, LAYERS)),
        dma((5, LAYERS, 3)),
        dma((5, LAYERS, 3)),
        dma((LAYERS, 7)),
        dma((LAYERS, 7)),
    ]
    spec = pl.BlockSpec(memory_space=pltpu.VMEM)

    def body(*refs):
        kernel(scale, *refs)

    act, grad, weight, bias = pl.pallas_call(
        body,
        name="encoder_sections",
        out_shape=(
            jax.ShapeDtypeStruct((micro, rows, nz), F32),
            jax.ShapeDtypeStruct((micro, rows, nz), F32),
            jax.ShapeDtypeStruct(weights.shape, F32),
            jax.ShapeDtypeStruct(biases.shape, F32),
        ),
        in_specs=[spec] * 4,
        out_specs=(spec,) * 4,
        scratch_shapes=scratch,
        compiler_params=pltpu.CompilerParams(
            collective_id=0, has_side_effects=True, vmem_limit_bytes=60 << 20
        ),
    )(
        inflow.reshape(micro, rows, nz),
        weights,
        biases,
        cotangent.reshape(micro, rows, nz),
    )
    shape = (1, micro, channels, nx, ny, nz)
    return act.reshape(shape), grad.reshape(shape), weight, bias


def solution(mesh):
    return jax.shard_map(
        per_device,
        mesh=mesh,
        in_specs=(
            P(None, None, None, "gy", "gz"),
            P("section", None, None, None),
            P("section", None),
            P(None, None, None, "gy", "gz"),
        ),
        out_specs=(
            P("section", None, None, None, "gy", "gz"),
            P("section", None, None, None, "gy", "gz"),
            P("section", None, None, None),
            P("section", None),
        ),
        check_vma=False,
    )
```

time: 1640 us -> 110 us (0.07)
  waiting for transfers between devices: 1060 us -> 0 us
  blocking collectives: 324 us -> 0 us
  starting transfers between devices: 137 us -> 0 us
  Pallas kernels: 0 us -> 102 us
  matrix products: 46.1 us -> 0 us
  between operations: 18 us -> 0.64 us
    psum x1 -> x0, waiting for transfers between devices: 935 us -> none  [per_device(): lax.psum((jnp.stack(weight_grads) * grad_scale, jnp.stack(bias_grads) * g...]
    psum x1 -> x0, blocking collectives: 324 us -> none  [per_device(): lax.psum((jnp.stack(weight_grads) * grad_scale, jnp.stack(bias_grads) * g...]
    ppermute x52 -> x0, starting transfers between devices: 137 us -> none  [the longest x24 77.4 us: extended(): lax.ppermute(lax.slice_in_dim(block, block.shape[dim] - width, None, axis...]
    ppermute x52 -> x0, waiting for transfers between devices: 129 us -> none  [the longest x24 84.5 us: extended(): lax.ppermute(lax.slice_in_dim(block, 0, width, axis=dim), axis, backward)]
    pallas_call x0 -> x1, Pallas kernels: none -> 102 us  [per_device(): pl.pallas_call(body, name='encoder_sections', out_shape=(jax.ShapeDtypeSt...]
    dot_general x18 -> x0, matrix products: 46.1 us -> none  [the longest x6 18 us: per_device(): jnp.einsum('oxyz,tcxyz->toc', slope_grad, stacked_taps(padded, extents, F...]
  transfers between devices with their start and end apart: 53 -> 0, of which waited for: 37 -> 0; matrix products, arithmetic and copies ran while one was open for 1% -> 0% of each run, Pallas kernels for 0% -> 0%
where the time goes in v1:
time: 110 us
  Pallas kernels  102 us (93%)
  local copies, waits for them, and re-layouts  6.79 us (6%)
    pallas_call x1, Pallas kernels, per_device(): pl.pallas_call(body, name='encoder_sections', out_shape=(jax.ShapeDtypeSt...  102 us
    unnamed x6, local copies, waits for them, and re-layouts  6.79 us

profile of v1, /device:TPU:1, one launch (start us, length us, event | category | flops | bytes accessed | tf_op | source)
XLA Modules:
  0.0 109.9 jit_solution(13622704891607664655)
XLA Ops:
  0.6 102.4 %encoder_sections.1 = (f32[2,256,128]{2,1,0:T(8,128)}, f32[2,256,128]{2,1,0:T(8,128)}, f32[2,27,64,64]{3,2,1,0:T(8,128)}, f32[2,64]{1,0:T(2,128)}) custom-call(f32[2,256,128]{2,1,0:T(8,128)} %bitcast.6, f32[2,27,64,64]{3,2,1,0:T(8,128)} %refs_1_.1, f32[2,64]{1,0:T(2,128)} %refs_2_.1, f32[2,256,128]{2,1,0:T(8,128)} %bitcast.7), custom_call_target="tpu_custom_call" | custom-call | tf_op jit(solution)/shard_map/encoder_sections/pallas_call | solution.py:694
  103.1 1.7 %copy.12 = f32[1,2,64,2,2,128]{5,4,3,2,1,0:T(2,128)} copy(f32[1,2,64,2,2,128]{5,4,3,2,1,0:T(2,128)} %bitcast.5) | data formatting | bytes 524288
  104.7 1.7 %copy.13 = f32[1,2,64,2,2,128]{5,4,3,2,1,0:T(2,128)} copy(f32[1,2,64,2,2,128]{5,4,3,2,1,0:T(2,128)} %bitcast.4) | data formatting | bytes 524288
  106.4 0.0 copy-start
  106.4 2.9 %copy.14 = f32[2,27,64,64]{3,2,1,0:T(8,128)} copy(f32[2,27,64,64]{3,2,1,0:T(8,128)} %get-tuple-element.18) | data formatting | bytes 1769472
  109.3 0.0 copy-done
  109.3 0.6 copy.15
Async XLA Ops:
  106.4 2.9 %copy-start = (f32[2,64]{1,0:T(2,128)S(1)}, f32[2,64]{1,0:T(2,128)}, u32[]{:S(2)}) copy-start(f32[2,64]{1,0:T(2,128)} %get-tuple-element.19) | copy-start | bytes 1540

commit v2 on v1

--- a/solution.py
+++ b/solution.py
@@ -17,6 +17,7 @@
 PACK = 880
 CHUNKS = 5
 CHUNK = PACK // 2 // CHUNKS
+EARLY = 3
 GRAD = 1024
 
 
@@ -43,14 +44,16 @@
 
 def kernel(
     scale,
+    inflow_hbm,
+    weights_hbm,
+    biases,
+    cotangent_hbm,
+    out_act,
+    out_grad,
+    final,
     inflow,
     weights,
-    biases,
     cotangent,
-    out_act,
-    out_grad,
-    out_weight,
-    out_bias,
     ext,
     patch,
     slope_patch,
@@ -61,7 +64,6 @@
     flow,
     stage,
     part,
-    final,
     half_in,
     half_sum,
     one_in,
@@ -69,6 +71,7 @@
     two_in,
     two_sum,
     three_in,
+    load_sem,
     halo_send,
     halo_recv,
     source_send,
@@ -104,9 +107,11 @@
         return (sec, new_gy, new_gz)
 
     mate = (sec, gy + 1 - 2 * core, gz)
-    step_sign = 1 - 2 * core
-    following = at_depth((depth + step_sign + 8) % 8, core)
-    at_end = zlo == 3 * (1 - core)
+    first_plane = zlo == 0
+    last_plane = zlo == 3
+    at_end = jnp.logical_or(first_plane, last_plane)
+    outward = at_depth((depth + jnp.where(last_plane, 1, 7)) % 8, core)
+    inward = at_depth((depth + jnp.where(last_plane, 7, 1)) % 8, core)
 
     def exists(dy, dz):
         ok = None
@@ -123,6 +128,61 @@
     def turned(value):
         return pltpu.roll(value, 64, 1)
 
+    loads = [
+        pltpu.make_async_copy(weights_hbm, weights, load_sem.at[0]),
+        pltpu.make_async_copy(inflow_hbm.at[sec], inflow, load_sem.at[1]),
+        pltpu.make_async_copy(cotangent_hbm.at[sec], cotangent, load_sem.at[2]),
+    ]
+    for load in loads:
+        load.start()
+
+    barrier = pltpu.get_barrier_semaphore()
+
+    def greet(device):
+        pl.semaphore_signal(barrier, inc=1, device_id=device, device_id_type=MESH)
+
+    for d in range(1, 8):
+        greet(at_depth((depth + d) % 8, core))
+    for d in range(1, 4):
+        greet((sec, gy + 2 * ((px + d) % 4 - px), gz))
+        greet((sec, gy, (gz + d) % 4))
+    for dy, dz in DIRS:
+        if dy != 0:
+
+            @pl.when(exists(dy, dz))
+            def _():
+                greet((sec, gy + dy, gz + dz))
+
+    sides_y = 2 - jnp.where(gy == 0, 1, 0) - jnp.where(gy == 31, 1, 0)
+    sides_z = 2 - jnp.where(gz == 0, 1, 0) - jnp.where(gz == 3, 1, 0)
+    def clear(rows, cells):
+        shape = (8, rows.size, cells.size, 128)
+        ext[:, rows, cells, :] = jnp.zeros(shape, F32)
+
+    @pl.when(gy == 0)
+    def _():
+        clear(pl.ds(0, 1), pl.ds(0, 144))
+
+    @pl.when(gy == 31)
+    def _():
+        clear(pl.ds(3, 1), pl.ds(0, 144))
+
+    @pl.when(gz == 0)
+    def _():
+        clear(pl.ds(0, 4), pl.ds(0, 8))
+
+    @pl.when(gz == 3)
+    def _():
+        clear(pl.ds(0, 4), pl.ds(136, 8))
+
+    def turned_in(ref, y):
+        rows = [ref[pl.ds(2 * x + y, 64, stride=4), :] for x in range(2)]
+        return jnp.concatenate(rows, axis=0).T
+
+    loads[1].wait()
+    for y in range(2):
+        ext[0, 1 + y, 8:136, :] = turned_in(inflow, y)
+    loads[0].wait()
     for i in range(2):
         for b in range(3):
             for c in range(3):
@@ -140,55 +200,6 @@
             jnp.concatenate([row, row], axis=1), (16, 128)
         )
 
-    def clear(rows, cells):
-        shape = (8, rows.size, cells.size, 128)
-        ext[:, rows, cells, :] = jnp.zeros(shape, F32)
-
-    @pl.when(gy == 0)
-    def _():
-        clear(pl.ds(0, 1), pl.ds(0, 144))
-
-    @pl.when(gy == 31)
-    def _():
-        clear(pl.ds(3, 1), pl.ds(0, 144))
-
-    @pl.when(gz == 0)
-    def _():
-        clear(pl.ds(0, 4), pl.ds(0, 8))
-
-    @pl.when(gz == 3)
-    def _():
-        clear(pl.ds(0, 4), pl.ds(136, 8))
-
-    def turned_in(ref, y):
-        rows = [ref[sec, pl.ds(2 * x + y, 64, stride=4), :] for x in range(2)]
-        return jnp.concatenate(rows, axis=0).T
-
-    for y in range(2):
-        ext[0, 1 + y, 8:136, :] = turned_in(inflow, y)
-        flow[y * 128 : (y + 1) * 128, :] = turned_in(cotangent, y)
-    for layer in range(LAYERS):
-        part[layer, 864:GRAD, :] = jnp.zeros((GRAD - 864, 128), F32)
-
-    barrier = pltpu.get_barrier_semaphore()
-
-    def greet(device):
-        pl.semaphore_signal(barrier, inc=1, device_id=device, device_id_type=MESH)
-
-    for d in range(1, 8):
-        greet(at_depth((depth + d) % 8, core))
-    for d in range(1, 4):
-        greet((sec, gy + 2 * ((px + d) % 4 - px), gz))
-        greet((sec, gy, (gz + d) % 4))
-    for dy, dz in DIRS:
-        if dy != 0:
-
-            @pl.when(exists(dy, dz))
-            def _():
-                greet((sec, gy + dy, gz + dz))
-
-    sides_y = 2 - jnp.where(gy == 0, 1, 0) - jnp.where(gy == 31, 1, 0)
-    sides_z = 2 - jnp.where(gz == 0, 1, 0) - jnp.where(gz == 3, 1, 0)
     pl.semaphore_wait(barrier, 13 + sides_y * (1 + sides_z))
 
     def send_rims(slot):
@@ -221,19 +232,22 @@
         start = parity * (PACK // 2) + chunk * CHUNK
         return packed.at[layer, pl.ds(pl.multiple_of(start, 8), CHUNK), :]
 
+    def pass_on(layer, i, chunk, send, recv, device):
+        piece = chunk_of(layer, core, chunk)
+        pltpu.make_async_remote_copy(
+            src_ref=piece,
+            dst_ref=piece,
+            send_sem=send.at[i, chunk],
+            recv_sem=recv.at[i, chunk],
+            device_id=device,
+            device_id_type=MESH,
+        ).start()
+
     @pl.when(at_end)
     def _():
         for i in range(2):
             for chunk in range(CHUNKS):
-                piece = chunk_of(2 * sec + i, core, chunk)
-                pltpu.make_async_remote_copy(
-                    src_ref=piece,
-                    dst_ref=piece,
-                    send_sem=source_send.at[i, chunk],
-                    recv_sem=relay_recv.at[i, chunk],
-                    device_id=following,
-                    device_id_type=MESH,
-                ).start()
+                pass_on(2 * sec + i, i, chunk, source_send, relay_recv, outward)
 
     def widen(layer):
         for tap in range(TAPS):
@@ -257,39 +271,30 @@
 
     lax.fori_loop(0, 2, widen_own, 0)
 
-    for i in range(2):
-        for chunk in range(CHUNKS):
-            piece = chunk_of(2 * other + i, core, chunk)
-            landed(piece, relay_recv.at[i, chunk])
-
-            @pl.when(jnp.logical_not(at_end))
-            def _():
-                pltpu.make_async_remote_copy(
-                    src_ref=piece,
-                    dst_ref=piece,
-                    send_sem=relay_send.at[i, chunk],
-                    recv_sem=relay_recv.at[i, chunk],
-                    device_id=following,
-                    device_id_type=MESH,
-                ).start()
-
-            pltpu.make_async_remote_copy(
-                src_ref=piece,
-                dst_ref=piece,
-                send_sem=mate_send.at[i, chunk],
-                recv_sem=mate_recv.at[i, chunk],
-                device_id=mate,
-                device_id_type=MESH,
-            ).start()
-    for i in range(2):
+    loads[2].wait()
+    for y in range(2):
+        flow[y * 128 : (y + 1) * 128, :] = turned_in(cotangent, y)
+    for layer in range(LAYERS):
+        part[layer, 864:GRAD, :] = jnp.zeros((GRAD - 864, 128), F32)
+
+    def relay(i, chunks):
+        for chunk in chunks:
+            landed(chunk_of(2 * other + i, core, chunk), relay_recv.at[i, chunk])
+
+            @pl.when(at_end)
+            def _():
+                pass_on(2 * other + i, i, chunk, relay_send, relay_recv, inward)
+
+            pass_on(2 * other + i, i, chunk, mate_send, mate_recv, mate)
+
+    def receive(i):
         for chunk in range(CHUNKS):
             landed(chunk_of(2 * other + i, 1 - core, chunk), mate_recv.at[i, chunk])
-
-    def widen_other(i, carry):
         widen(2 * other + i)
-        return carry
-
-    lax.fori_loop(0, 2, widen_other, 0)
+
+    relay(0, range(CHUNKS))
+    receive(0)
+    relay(1, range(EARLY))
 
     def fill(slot, store):
         for c in range(3):
@@ -358,6 +363,11 @@
                 ext[layer + 1, 1 + y, 8:136, :] = active[y * 128 : (y + 1) * 128, :]
             send_rims(layer + 1)
 
+        @pl.when(layer == 0)
+        def _():
+            relay(1, range(EARLY, CHUNKS))
+            receive(1)
+
         @pl.when(layer == 1)
         def _():
             hand_out(active, 0, 0, out_act)
@@ -375,7 +385,6 @@
     offset_half = core * 512
     offset_one = offset_half + index_one * 128
     offset_two = offset_one + index_two * 32
-    offset_three = offset_two + zlo * 8
 
     def rows_at(ref, layer, start, size):
         return ref.at[layer, pl.ds(pl.multiple_of(start, 8), size), :]
@@ -440,81 +449,60 @@
             @pl.when(peer // 4 == layer // 2)
             def _():
                 push(
-                    rows_at(two_sum, layer, (peer % 4) * 8, 8),
-                    three_in.at[layer, 7 - d],
-                    deep_send.at[layer, 7 - d],
-                    deep_recv.at[layer, 7 - d],
+                    two_sum.at[layer],
+                    three_in.at[layer, depth],
+                    deep_send.at[layer, d - 1],
+                    deep_recv.at[layer, d - 1],
                     at_depth(peer, core),
                 )
 
-    def gather_three(layer):
-        for s in range(7):
-            landed(three_in.at[layer, s], deep_recv.at[layer, s])
-        total = two_sum[layer, pl.ds(pl.multiple_of(zlo * 8, 8), 8), :]
-        for s in range(7):
-            total = total + three_in[layer, s]
-        start = pl.multiple_of(offset_three, 8)
-        final[layer, pl.ds(start, 8), :] = total * scale
+    def gathered(layer, stage_at, base, index, size):
+        for s in range(3):
+            sender = (index + 1 + s) % 4
+            piece = rows_at(final, layer % 2, base + sender * size, size)
+            landed(piece, group_recv.at[stage_at, layer, s])
+
+    def gather_two(layer):
+        for d in range(1, 8):
+            landed(three_in.at[layer, (depth + 8 - d) % 8], deep_recv.at[layer, d - 1])
+        three_in[layer, depth] = two_sum[layer]
+        total = three_in[layer, 0]
+        for level in range(1, 8):
+            total = total + three_in[layer, level]
+        final[layer % 2, pl.ds(pl.multiple_of(offset_two, 8), 32), :] = total * scale
         for d in range(1, 4):
-            piece = rows_at(final, layer, offset_three, 8)
+            piece = rows_at(final, layer % 2, offset_two, 32)
             push(
                 piece,
                 piece,
                 group_send.at[2, layer, 3 - d],
                 group_recv.at[2, layer, 3 - d],
-                at_depth(sec * 4 + (zlo + d) % 4, core),
+                in_plane(False, (index_two + d) % 4),
             )
 
-    def gathered(layer, stage_at, base, index, size):
-        for s in range(3):
-            sender = (index + 1 + s) % 4
-            piece = rows_at(final, layer, base + sender * size, size)
-            landed(piece, group_recv.at[stage_at, layer, s])
-
-    def gather_two(layer):
-        gathered(layer, 2, offset_two, zlo, 8)
+    def gather_one(layer):
+        gathered(layer, 2, offset_one, index_two, 32)
         for d in range(1, 4):
-            piece = rows_at(final, layer, offset_two, 32)
+            piece = rows_at(final, layer % 2, offset_one, 128)
             push(
                 piece,
                 piece,
                 group_send.at[3, layer, 3 - d],
                 group_recv.at[3, layer, 3 - d],
-                in_plane(False, (index_two + d) % 4),
-            )
-
-    def gather_one(layer):
-        gathered(layer, 3, offset_one, index_two, 32)
-        for d in range(1, 4):
-            piece = rows_at(final, layer, offset_one, 128)
-            push(
-                piece,
-                piece,
-                group_send.at[4, layer, 3 - d],
-                group_recv.at[4, layer, 3 - d],
                 in_plane(True, (index_one + d) % 4),
             )
 
     def gather_half(layer):
-        gathered(layer, 4, offset_half, index_one, 128)
-        piece = rows_at(final, layer, offset_half, 512)
+        gathered(layer, 3, offset_half, index_one, 128)
+        piece = rows_at(final, layer % 2, offset_half, 512)
         push(piece, piece, pair_send.at[1, layer], pair_recv.at[1, layer], mate)
 
-    def unpack(layer):
-        i = layer % 2
-        landed(rows_at(final, layer, (1 - core) * 512, 512), pair_recv.at[1, layer])
-        for tap in range(TAPS):
-            base = tap * TAP_ROWS
-            top = final[layer, base : base + 64, :]
-            near = final[layer, base + 64 : base + 96, :]
-            out_weight[i, 9 + tap] = top[:, 0:64]
-            out_weight[i, 18 + tap] = turned(top)[:, 0:64]
-            out_weight[i, tap, 0:32, :] = near[:, 0:64]
-            out_weight[i, tap, 32:64, :] = turned(near)[:, 0:64]
-        out_bias[i : i + 1, :] = final[layer, 864:865, 0:64]
+    def finish(layer):
+        piece = rows_at(final, layer % 2, (1 - core) * 512, 512)
+        landed(piece, pair_recv.at[1, layer])
 
     everywhere = [reduce_half, reduce_one, reduce_two]
-    at_home = [gather_three, gather_two, gather_one, gather_half, unpack]
+    at_home = [gather_two, gather_one, gather_half, finish]
 
     def backward(step, carry):
         layer = LAYERS - 1 - step
@@ -579,12 +567,12 @@
 
     lax.fori_loop(0, LAYERS, backward, 0)
 
-    for round_at in range(8):
+    for round_at in range(7):
         for layer in reversed(range(LAYERS)):
             tick = layer + round_at
             if tick < 3:
                 everywhere[tick](layer)
-            elif tick < 8:
+            elif tick < 7:
 
                 @pl.when(sec == layer // 2)
                 def _():
@@ -611,7 +599,7 @@
             def _():
                 landed(chunk_of(2 * sec + i, core, chunk), source_send.at[i, chunk])
 
-            @pl.when(jnp.logical_not(at_end))
+            @pl.when(at_end)
             def _():
                 landed(chunk_of(2 * other + i, core, chunk), relay_send.at[i, chunk])
 
@@ -629,19 +617,41 @@
 
             @pl.when(((depth + d) % 8) // 4 == layer // 2)
             def _():
-                landed(three_in.at[layer, 7 - d], deep_send.at[layer, 7 - d])
+                landed(two_sum.at[layer], deep_send.at[layer, d - 1])
 
         @pl.when(home)
         def _():
             for s in range(3):
-                landed(three_in.at[layer, s], group_send.at[2, layer, s])
-                landed(two_in.at[layer, s], group_send.at[3, layer, s])
-                landed(one_in.at[layer, s], group_send.at[4, layer, s])
+                landed(two_in.at[layer, s], group_send.at[2, layer, s])
+                landed(one_in.at[layer, s], group_send.at[3, layer, s])
             landed(half_in.at[layer], pair_send.at[1, layer])
 
         return carry
 
     lax.fori_loop(0, LAYERS, drain_sums, 0)
+
+
+def unpack(act, grad, total, out_act, out_grad, out_weight, out_bias, spread, sem):
+    copies = [
+        pltpu.make_async_copy(act, out_act, sem.at[0]),
+        pltpu.make_async_copy(grad, out_grad, sem.at[1]),
+    ]
+    for copy in copies:
+        copy.start()
+    for i in range(2):
+        for tap in range(TAPS):
+            base = tap * TAP_ROWS
+            top = total[i, base : base + 64, :]
+            near = total[i, base + 64 : base + 96, :]
+            spread[i, 9 + tap] = top[:, 0:64]
+            spread[i, 18 + tap] = pltpu.roll(top, 64, 1)[:, 0:64]
+            spread[i, tap, 0:32, :] = near[:, 0:64]
+            spread[i, tap, 32:64, :] = pltpu.roll(near, 64, 1)[:, 0:64]
+        copies.append(pltpu.make_async_copy(spread.at[i], out_weight.at[i], sem.at[2 + i]))
+        copies[-1].start()
+    out_bias[...] = total[:, 864, 0:64]
+    for copy in copies:
+        copy.wait()
 
 
 def per_device(inflow, weights, biases, cotangent):
@@ -652,6 +662,9 @@
     vmem = pltpu.VMEM
     dma = pltpu.SemaphoreType.DMA
     scratch = [
+        vmem((rows, nz), F32),
+        vmem(weights.shape, F32),
+        vmem((rows, nz), F32),
         vmem((8, 4, 144, 128), F32),
         vmem((LAYERS, 512, TAPS * 128), BF16),
         vmem((512, TAPS * 128), BF16),
@@ -662,14 +675,14 @@
         vmem((256, 128), F32),
         vmem((2, 256, 128), F32),
         vmem((LAYERS, GRAD, 128), F32),
-        vmem((LAYERS, GRAD, 128), F32),
         vmem((LAYERS, 512, 128), F32),
         vmem((LAYERS, 512, 128), F32),
         vmem((LAYERS, 3, 128, 128), F32),
         vmem((LAYERS, 128, 128), F32),
         vmem((LAYERS, 3, 32, 128), F32),
         vmem((LAYERS, 32, 128), F32),
-        vmem((LAYERS, 7, 8, 128), F32),
+        vmem((LAYERS, 8, 32, 128), F32),
+        dma((3,)),
         dma((8, 8)),
         dma((8, 8)),
         dma((2, CHUNKS)),
@@ -681,30 +694,30 @@
         dma((2,)),
         dma((2, LAYERS)),
         dma((2, LAYERS)),
-        dma((5, LAYERS, 3)),
-        dma((5, LAYERS, 3)),
+        dma((4, LAYERS, 3)),
+        dma((4, LAYERS, 3)),
         dma((LAYERS, 7)),
         dma((LAYERS, 7)),
     ]
-    spec = pl.BlockSpec(memory_space=pltpu.VMEM)
+    near = pl.BlockSpec(memory_space=pltpu.VMEM)
+    far = pl.BlockSpec(memory_space=pl.ANY)
 
     def body(*refs):
         kernel(scale, *refs)
 
-    act, grad, weight, bias = pl.pallas_call(
+    act, grad, total = pl.pallas_call(
         body,
         name="encoder_sections",
         out_shape=(
-            jax.ShapeDtypeStruct((micro, rows, nz), F32),
-            jax.ShapeDtypeStruct((micro, rows, nz), F32),
-            jax.ShapeDtypeStruct(weights.shape, F32),
-            jax.ShapeDtypeStruct(biases.shape, F32),
+            vmem((micro, rows, nz), F32),
+            vmem((micro, rows, nz), F32),
+            vmem((2, GRAD, 128), F32),
         ),
-        in_specs=[spec] * 4,
-        out_specs=(spec,) * 4,
+        in_specs=[far, far, near, far],
+        out_specs=(near,) * 3,
         scratch_shapes=scratch,
         compiler_params=pltpu.CompilerParams(
-            collective_id=0, has_side_effects=True, vmem_limit_bytes=60 << 20
+            collective_id=0, has_side_effects=True, vmem_limit_bytes=56 << 20
         ),
     )(
         inflow.reshape(micro, rows, nz),
@@ -712,6 +725,20 @@
         biases,
         cotangent.reshape(micro, rows, nz),
     )
+    act, grad, weight, bias = pl.pallas_call(
+        unpack,
+        name="write_results",
+        out_shape=(
+            jax.ShapeDtypeStruct(act.shape, F32),
+            jax.ShapeDtypeStruct(grad.shape, F32),
+            jax.ShapeDtypeStruct(weights.shape, F32),
+            jax.ShapeDtypeStruct(biases.shape, F32),
+        ),
+        in_specs=[near] * 3,
+        out_specs=(far, far, far, near),
+        scratch_shapes=[vmem(weights.shape, F32), dma((4,))],
+        compiler_params=pltpu.CompilerParams(vmem_limit_bytes=8 << 20),
+    )(act, grad, total)
     shape = (1, micro, channels, nx, ny, nz)
     return act.reshape(shape), grad.reshape(shape), weight, bias
 

time: 110 us -> 99.9 us (0.908)
  local copies, waits for them, and re-layouts: 6.79 us -> 0 us
  Pallas kernels: 102 us -> 99.1 us
    unnamed x6 -> x0, local copies, waits for them, and re-layouts: 6.79 us -> none
    pallas_call x1 -> x2, Pallas kernels: 102 us -> 99.1 us  [the longest x1 97.1 us: per_device(): pl.pallas_call(body, name='encoder_sections', out_shape=(vmem((micro, row...]
where the time goes in v2:
time: 99.9 us; the launch traced here: 99.7 us
  Pallas kernels  99.1 us (99%)
    pallas_call x1, Pallas kernels, per_device(): pl.pallas_call(body, name='encoder_sections', out_shape=(vmem((micro, row...  97.1 us

profile of v2, /device:TPU:1, one launch (start us, length us, event | category | flops | bytes accessed | tf_op | source)
XLA Modules:
  0.0 99.7 jit_solution(11576688172629529108)
XLA Ops:
  0.6 97.1 %encoder_sections.1 = (f32[2,256,128]{2,1,0:T(8,128)S(1)}, f32[2,256,128]{2,1,0:T(8,128)S(1)}, f32[2,1024,128]{2,1,0:T(8,128)S(1)}) custom-call(f32[2,256,128]{2,1,0:T(8,128)} %bitcast.4, f32[2,27,64,64]{3,2,1,0:T(8,128)} %refs_1_.1, f32[2,64]{1,0:T(2,128)} %refs_2_.1, f32[2,256,128]{2,1,0:T(8,128)} %bitcast.5), custom_call_target="tpu_custom_call" | custom-call | tf_op jit(solution)/shard_map/encoder_sections/pallas_call | solution.py:708
  97.8 2.0 %write_results.1 = (f32[2,256,128]{2,1,0:T(8,128)}, f32[2,256,128]{2,1,0:T(8,128)}, f32[2,27,64,64]{3,2,1,0:T(8,128)}, f32[2,64]{1,0:T(2,128)}) custom-call(f32[2,256,128]{2,1,0:T(8,128)S(1)} %get-tuple-element.11.act, f32[2,256,128]{2,1,0:T(8,128)S(1)} %get-tuple-element.12.grad, f32[2,1024,128]{2,1,0:T(8,128)S(1)} %get-tuple-element.13.total), custom_call_target="tpu_custom_call" | custom-call | tf_op jit(solution)/shard_map/write_results/pallas_call | solution.py:728

commit v3 on v2

--- a/solution.py
+++ b/solution.py
@@ -19,6 +19,7 @@
 CHUNK = PACK // 2 // CHUNKS
 EARLY = 3
 GRAD = 1024
+WIDE = 576
 
 
 def split_parts(value):
@@ -27,14 +28,13 @@
 
 
 def source_window(dy, dz):
-    rows = {1: pl.ds(2, 1), -1: pl.ds(1, 1), 0: pl.ds(1, 2)}[dy]
-    cells = {1: pl.ds(128, 8), -1: pl.ds(8, 8), 0: pl.ds(8, 128)}[dz]
-    return rows, cells
+    cells = {1: pl.ds(136, 8), -1: pl.ds(16, 8), 0: pl.ds(16, 128)}[dz]
+    return pl.ds(2, 2), cells
 
 
 def target_window(dy, dz):
-    rows = {1: pl.ds(0, 1), -1: pl.ds(3, 1), 0: pl.ds(1, 2)}[dy]
-    cells = {1: pl.ds(0, 8), -1: pl.ds(136, 8), 0: pl.ds(8, 128)}[dz]
+    rows = {1: pl.ds(0, 2), -1: pl.ds(4, 2), 0: pl.ds(2, 2)}[dy]
+    cells = {1: pl.ds(8, 8), -1: pl.ds(144, 8), 0: pl.ds(16, 128)}[dz]
     return rows, cells
 
 
@@ -55,11 +55,14 @@
     weights,
     cotangent,
     ext,
+    inner,
+    wide_patch,
     patch,
     slope_patch,
     wide_f,
     wide_b,
     packed,
+    wide_pre,
     pre,
     flow,
     stage,
@@ -156,24 +159,26 @@
     sides_y = 2 - jnp.where(gy == 0, 1, 0) - jnp.where(gy == 31, 1, 0)
     sides_z = 2 - jnp.where(gz == 0, 1, 0) - jnp.where(gz == 3, 1, 0)
     def clear(rows, cells):
-        shape = (8, rows.size, cells.size, 128)
-        ext[:, rows, cells, :] = jnp.zeros(shape, F32)
+        ext[:, rows, cells, :] = jnp.zeros((4, rows.size, cells.size, 128), F32)
+
+    clear(pl.ds(0, 6), pl.ds(0, 8))
+    clear(pl.ds(0, 6), pl.ds(152, 8))
 
     @pl.when(gy == 0)
     def _():
-        clear(pl.ds(0, 1), pl.ds(0, 144))
+        clear(pl.ds(0, 2), pl.ds(8, 144))
 
     @pl.when(gy == 31)
     def _():
-        clear(pl.ds(3, 1), pl.ds(0, 144))
+        clear(pl.ds(4, 2), pl.ds(8, 144))
 
     @pl.when(gz == 0)
     def _():
-        clear(pl.ds(0, 4), pl.ds(0, 8))
+        clear(pl.ds(0, 6), pl.ds(8, 8))
 
     @pl.when(gz == 3)
     def _():
-        clear(pl.ds(0, 4), pl.ds(136, 8))
+        clear(pl.ds(0, 6), pl.ds(144, 8))
 
     def turned_in(ref, y):
         rows = [ref[pl.ds(2 * x + y, 64, stride=4), :] for x in range(2)]
@@ -181,7 +186,7 @@
 
     loads[1].wait()
     for y in range(2):
-        ext[0, 1 + y, 8:136, :] = turned_in(inflow, y)
+        ext[0, 2 + y, 16:144, :] = turned_in(inflow, y)
     loads[0].wait()
     for i in range(2):
         for b in range(3):
@@ -296,15 +301,55 @@
     receive(0)
     relay(1, range(EARLY))
 
-    def fill(slot, store):
+    def reach(condition):
+        return lane < jnp.where(condition, 128, 0)
+
+    inside_low, inside_high = reach(gz > 0), reach(gz < 3)
+    inside_line = [reach(gy > 0), None, None, reach(gy < 31)]
+
+    def fill_wide(slot, put):
+        for c in range(3):
+            for row in range(6):
+                line = ext[slot, row, 15 + c : 143 + c, :]
+                edge = jnp.concatenate(
+                    [ext[slot, row, 7 + c : 15 + c, :], ext[slot, row, 143 + c : 151 + c, :]],
+                    axis=0,
+                )
+                parts = zip(split_parts(line), split_parts(edge))
+                for at, (line_part, edge_part) in enumerate(parts):
+                    for y in range(4):
+                        b = row - y
+                        if 0 <= b <= 2:
+                            cols = slice((b * 3 + c) * 128, (b * 3 + c) * 128 + 128)
+                            start = at * WIDE + y * 128
+                            put(slice(start, start + 128), cols, line_part)
+                            start = at * WIDE + 512 + y * 16
+                            put(slice(start, start + 16), cols, edge_part)
+
+    def fill_inner(put):
         for c in range(3):
             for row in range(4):
-                high, low = split_parts(ext[slot, row, 7 + c : 135 + c, :])
-                for y in range(2):
-                    b = row - y
-                    if 0 <= b <= 2:
-                        tap = b * 3 + c
-                        store(y, tap, high, low)
+                line = inner[row, 15 + c : 143 + c, :]
+                for at, line_part in enumerate(split_parts(line)):
+                    for y in range(2):
+                        b = row - y
+                        if 0 <= b <= 2:
+                            cols = slice((b * 3 + c) * 128, (b * 3 + c) * 128 + 128)
+                            start = at * 256 + y * 128
+                            put(slice(start, start + 128), cols, line_part)
+
+    def keep_inner(value):
+        for y in range(4):
+            line = value[y * 128 : (y + 1) * 128, :]
+            low = value[512 + y * 16 : 520 + y * 16, :]
+            high = value[520 + y * 16 : 528 + y * 16, :]
+            low = jnp.where(inside_low, low, 0.0)
+            high = jnp.where(inside_high, high, 0.0)
+            if inside_line[y] is not None:
+                line, low, high = (jnp.where(inside_line[y], v, 0.0) for v in (line, low, high))
+            inner[y, 16:144, :] = line
+            inner[y, 8:16, :] = low
+            inner[y, 144:152, :] = high
 
     def hand_out(value, keeper, kind, result):
         def put(ref, lead):
@@ -331,54 +376,69 @@
             ).start()
 
     def joined(product):
-        return (
-            product[0:256, 0:128]
-            + product[0:256, 128:256]
-            + product[256:512, 0:128]
-            + product[256:512, 128:256]
+        cells = product.shape[0] // 2
+        return (product[:cells, 0:128] + product[:cells, 128:256]) + (
+            product[cells:, 0:128] + product[cells:, 128:256]
         )
 
-    def forward(layer, carry):
-        await_rims(layer)
-
-        def store(y, tap, high, low):
-            cols = slice(tap * 128, tap * 128 + 128)
-            patch[layer, y * 128 : y * 128 + 128, cols] = high
-            patch[layer, 256 + y * 128 : 384 + y * 128, cols] = low
-
-        fill(layer, store)
+    def across(patches, layer):
         product = lax.dot_general(
-            patch[layer],
-            wide_f[layer],
-            (((1,), (1,)), ((), ())),
-            preferred_element_type=F32,
+            patches, wide_f[layer], (((1,), (1,)), ((), ())), preferred_element_type=F32
         )
-        value = joined(product) + packed[layer, 864:865, :]
-        pre[layer] = value
-        active = value * (1.0 / (1.0 + jnp.exp(-value)))
-
-        @pl.when(layer < LAYERS - 1)
-        def _():
-            for y in range(2):
-                ext[layer + 1, 1 + y, 8:136, :] = active[y * 128 : (y + 1) * 128, :]
-            send_rims(layer + 1)
-
-        @pl.when(layer == 0)
+        return joined(product) + packed[layer, 864:865, :]
+
+    def back_across(patches, layer):
+        return joined(jnp.dot(patches, wide_b[layer], preferred_element_type=F32))
+
+    def active(value):
+        return value * (1.0 / (1.0 + jnp.exp(-value)))
+
+    def slope_of(gradient, value):
+        sigma = 1.0 / (1.0 + jnp.exp(-value))
+        return gradient * sigma * (1.0 + value * (1.0 - sigma))
+
+    def keep_own(slot, value):
+        for y in range(2):
+            ext[slot, 2 + y, 16:144, :] = value[y * 128 : (y + 1) * 128, :]
+
+    def forward(pair, carry):
+        first = 2 * pair
+        await_rims(pair)
+
+        def put_wide(rows, cols, value):
+            wide_patch[pair, rows, cols] = value
+
+        fill_wide(pair, put_wide)
+        value = across(wide_patch[pair], first)
+        wide_pre[pair] = value
+        keep_inner(active(value))
+
+        @pl.when(pair == 0)
         def _():
             relay(1, range(EARLY, CHUNKS))
             receive(1)
 
-        @pl.when(layer == 1)
-        def _():
-            hand_out(active, 0, 0, out_act)
-
-        @pl.when(layer == 3)
-        def _():
-            hand_out(active, 1, 0, out_act)
+        def put(rows, cols, value):
+            patch[pair, rows, cols] = value
+
+        fill_inner(put)
+        value = across(patch[pair], first + 1)
+        pre[pair] = value
+        result = active(value)
+
+        @pl.when(pair == 0)
+        def _():
+            keep_own(1, result)
+            send_rims(1)
+            hand_out(result, 0, 0, out_act)
+
+        @pl.when(pair == 1)
+        def _():
+            hand_out(result, 1, 0, out_act)
 
         return carry
 
-    lax.fori_loop(0, LAYERS, forward, 0)
+    lax.fori_loop(0, 2, forward, 0)
 
     index_one = px + core * (gz - px)
     index_two = gz + core * (px - gz)
@@ -504,26 +564,12 @@
     everywhere = [reduce_half, reduce_one, reduce_two]
     at_home = [gather_two, gather_one, gather_half, finish]
 
-    def backward(step, carry):
-        layer = LAYERS - 1 - step
-        slot = LAYERS + layer
-        value = pre[layer]
-        sigma = 1.0 / (1.0 + jnp.exp(-value))
-        slope = flow[...] * sigma * (1.0 + value * (1.0 - sigma))
-        for y in range(2):
-            ext[slot, 1 + y, 8:136, :] = slope[y * 128 : (y + 1) * 128, :]
-        send_rims(slot)
-
-        across = jnp.concatenate([slope[0:128, :].T, slope[128:256, :].T], axis=1)
-        high, low = split_parts(across)
-        sides = jnp.concatenate(
-            [
-                jnp.concatenate([high, high], axis=1),
-                jnp.concatenate([low, low], axis=1),
-            ],
-            axis=0,
+    def weigh(layer, slope, high_patch, low_patch):
+        turned_slope = jnp.concatenate([slope[0:128, :].T, slope[128:256, :].T], axis=1)
+        sides = jnp.concatenate(split_parts(turned_slope), axis=0)
+        product = jnp.dot(sides, high_patch, preferred_element_type=F32) + jnp.dot(
+            sides, low_patch, preferred_element_type=F32
         )
-        product = jnp.dot(sides, patch[layer], preferred_element_type=F32)
         for tap in range(TAPS):
             cols = slice(tap * 128, tap * 128 + 128)
             block = product[0:128, cols] + product[128:256, cols]
@@ -536,36 +582,61 @@
         sums = jnp.sum(slope, axis=0, keepdims=True)
         part[layer, 864:865, :] = sums + turned(sums)
         reduce_start(layer)
-        for k, tick in enumerate(everywhere):
-
-            @pl.when(layer + k + 1 < LAYERS)
-            def _():
-                tick(layer + k + 1)
+
+    def put_slope(rows, cols, value):
+        slope_patch[rows, cols] = value
+
+    def backward(step, carry):
+        pair = 1 - step
+        first = 2 * pair
+        slot = 2 + step
+        slope = slope_of(flow[...], pre[pair])
+        keep_own(slot, slope)
+        send_rims(slot)
+        weigh(first + 1, slope, patch[pair, 0:256, :], patch[pair, 256:512, :])
+
+        @pl.when(pair == 0)
+        def _():
+            reduce_half(2)
+            reduce_one(3)
 
         await_rims(slot)
-
-        def store(y, tap, high, low):
-            cols = slice(tap * 128, tap * 128 + 128)
-            slope_patch[y * 128 : y * 128 + 128, cols] = high
-            slope_patch[256 + y * 128 : 384 + y * 128, cols] = low
-
-        fill(slot, store)
-        gradient = joined(
-            jnp.dot(slope_patch[...], wide_b[layer], preferred_element_type=F32)
+        fill_wide(slot, put_slope)
+        gradient = back_across(slope_patch[...], first + 1)
+        slope = slope_of(gradient, wide_pre[pair])
+        keep_inner(slope)
+        weigh(
+            first,
+            slope[128:384, :],
+            wide_patch[pair, 128:384, :],
+            wide_patch[pair, WIDE + 128 : WIDE + 384, :],
         )
+
+        @pl.when(pair == 1)
+        def _():
+            reduce_half(3)
+
+        @pl.when(pair == 0)
+        def _():
+            reduce_half(1)
+            reduce_one(2)
+            reduce_two(3)
+
+        fill_inner(put_slope)
+        gradient = back_across(slope_patch[0:512, :], first)
         flow[...] = gradient
 
-        @pl.when(layer == 2)
+        @pl.when(pair == 1)
         def _():
             hand_out(gradient, 1, 1, out_grad)
 
-        @pl.when(layer == 0)
+        @pl.when(pair == 0)
         def _():
             hand_out(gradient, 0, 1, out_grad)
 
         return carry
 
-    lax.fori_loop(0, LAYERS, backward, 0)
+    lax.fori_loop(0, 2, backward, 0)
 
     for round_at in range(7):
         for layer in reversed(range(LAYERS)):
@@ -591,7 +662,7 @@
 
         return carry
 
-    lax.fori_loop(0, 8, drain_rims, 0)
+    lax.fori_loop(0, 4, drain_rims, 0)
     for i in range(2):
         for chunk in range(CHUNKS):
 
@@ -665,13 +736,16 @@
         vmem((rows, nz), F32),
         vmem(weights.shape, F32),
         vmem((rows, nz), F32),
-        vmem((8, 4, 144, 128), F32),
-        vmem((LAYERS, 512, TAPS * 128), BF16),
-        vmem((512, TAPS * 128), BF16),
+        vmem((4, 6, 160, 128), F32),
+        vmem((4, 160, 128), F32),
+        vmem((2, 2 * WIDE, TAPS * 128), BF16),
+        vmem((2, 512, TAPS * 128), BF16),
+        vmem((2 * WIDE, TAPS * 128), BF16),
         vmem((LAYERS, 256, TAPS * 128), BF16),
         vmem((LAYERS, TAPS * 128, 256), BF16),
         vmem((LAYERS, PACK, 128), F32),
-        vmem((LAYERS, 256, 128), F32),
+        vmem((2, WIDE, 128), F32),
+        vmem((2, 256, 128), F32),
         vmem((256, 128), F32),
         vmem((2, 256, 128), F32),
         vmem((LAYERS, GRAD, 128), F32),
@@ -683,8 +757,8 @@
         vmem((LAYERS, 32, 128), F32),
         vmem((LAYERS, 8, 32, 128), F32),
         dma((3,)),
-        dma((8, 8)),
-        dma((8, 8)),
+        dma((4, 8)),
+        dma((4, 8)),
         dma((2, CHUNKS)),
         dma((2, CHUNKS)),
         dma((2, CHUNKS)),

time: 99.9 us -> 92.7 us (0.928)
  Pallas kernels: 99.1 us -> 92 us
    pallas_call x1, Pallas kernels: 97.1 us -> 90 us  [per_device(): pl.pallas_call(body, name='encoder_sections', out_shape=(vmem((micro, row...]
where the time goes in v3:
time: 92.7 us; the launch traced here: 92.6 us
  Pallas kernels  92 us (99%)
    pallas_call x1, Pallas kernels, per_device(): pl.pallas_call(body, name='encoder_sections', out_shape=(vmem((micro, row...  90 us
    pallas_call x1, Pallas kernels, per_device(): pl.pallas_call(unpack, name='write_results', out_shape=(jax.ShapeDtypeStr...  1.99 us

profile of v3, /device:TPU:1, one launch (start us, length us, event | category | flops | bytes accessed | tf_op | source)
XLA Modules:
  0.0 92.6 jit_solution(14256884096726108817)
XLA Ops:
  0.6 90.0 %encoder_sections.1 = (f32[2,256,128]{2,1,0:T(8,128)S(1)}, f32[2,256,128]{2,1,0:T(8,128)S(1)}, f32[2,1024,128]{2,1,0:T(8,128)S(1)}) custom-call(f32[2,256,128]{2,1,0:T(8,128)} %bitcast.4, f32[2,27,64,64]{3,2,1,0:T(8,128)} %refs_1_.1, f32[2,64]{1,0:T(2,128)} %refs_2_.1, f32[2,256,128]{2,1,0:T(8,128)} %bitcast.5), custom_call_target="tpu_custom_call" | custom-call | tf_op jit(solution)/shard_map/encoder_sections/pallas_call | solution.py:782
  90.6 2.0 %write_results.1 = (f32[2,256,128]{2,1,0:T(8,128)}, f32[2,256,128]{2,1,0:T(8,128)}, f32[2,27,64,64]{3,2,1,0:T(8,128)}, f32[2,64]{1,0:T(2,128)}) custom-call(f32[2,256,128]{2,1,0:T(8,128)S(1)} %get-tuple-element.11.act, f32[2,256,128]{2,1,0:T(8,128)S(1)} %get-tuple-element.12.grad, f32[2,1024,128]{2,1,0:T(8,128)S(1)} %get-tuple-element.13.total), custom_call_target="tpu_custom_call" | custom-call | tf_op jit(solution)/shard_map/write_results/pallas_call | solution.py:802

commit v4 on v3

--- a/solution.py
+++ b/solution.py
@@ -56,9 +56,11 @@
     cotangent,
     ext,
     inner,
-    wide_patch,
-    patch,
-    slope_patch,
+    wide_lines,
+    wide_rims,
+    lines,
+    slope_lines,
+    slope_rims,
     wide_f,
     wide_b,
     packed,
@@ -66,6 +68,7 @@
     pre,
     flow,
     stage,
+    midway,
     part,
     half_in,
     half_sum,
@@ -84,6 +87,8 @@
     mate_recv,
     out_send,
     out_recv,
+    mid_send,
+    mid_recv,
     pair_send,
     pair_recv,
     group_send,
@@ -307,7 +312,7 @@
     inside_low, inside_high = reach(gz > 0), reach(gz < 3)
     inside_line = [reach(gy > 0), None, None, reach(gy < 31)]
 
-    def fill_wide(slot, put):
+    def fill_wide(slot, line_ref, edge_ref):
         for c in range(3):
             for row in range(6):
                 line = ext[slot, row, 15 + c : 143 + c, :]
@@ -315,28 +320,37 @@
                     [ext[slot, row, 7 + c : 15 + c, :], ext[slot, row, 143 + c : 151 + c, :]],
                     axis=0,
                 )
-                parts = zip(split_parts(line), split_parts(edge))
-                for at, (line_part, edge_part) in enumerate(parts):
-                    for y in range(4):
-                        b = row - y
-                        if 0 <= b <= 2:
-                            cols = slice((b * 3 + c) * 128, (b * 3 + c) * 128 + 128)
-                            start = at * WIDE + y * 128
-                            put(slice(start, start + 128), cols, line_part)
-                            start = at * WIDE + 512 + y * 16
-                            put(slice(start, start + 16), cols, edge_part)
-
-    def fill_inner(put):
+                for at, value in enumerate(split_parts(line)):
+                    line_ref[at, c, row * 128 : row * 128 + 128, :] = value
+                for at, value in enumerate(split_parts(edge)):
+                    edge_ref[at, c, row * 16 : row * 16 + 16, :] = value
+
+    def fill_inner(line_ref):
         for c in range(3):
             for row in range(4):
                 line = inner[row, 15 + c : 143 + c, :]
-                for at, line_part in enumerate(split_parts(line)):
-                    for y in range(2):
-                        b = row - y
-                        if 0 <= b <= 2:
-                            cols = slice((b * 3 + c) * 128, (b * 3 + c) * 128 + 128)
-                            start = at * 256 + y * 128
-                            put(slice(start, start + 128), cols, line_part)
+                for at, value in enumerate(split_parts(line)):
+                    line_ref[at, c, row * 128 : row * 128 + 128, :] = value
+
+    def taps_of(ref, at, size, first, count):
+        return jnp.concatenate(
+            [
+                ref[at, c, (first + b) * size : (first + b + count) * size, :]
+                for b in range(3)
+                for c in range(3)
+            ],
+            axis=1,
+        )
+
+    def wide_taps(line_ref, edge_ref):
+        blocks = []
+        for at in range(2):
+            blocks.append(taps_of(line_ref, at, 128, 0, 4))
+            blocks.append(taps_of(edge_ref, at, 16, 0, 4))
+        return jnp.concatenate(blocks, axis=0)
+
+    def inner_taps(line_ref):
+        return jnp.concatenate([taps_of(line_ref, at, 128, 0, 2) for at in range(2)], axis=0)
 
     def keep_inner(value):
         for y in range(4):
@@ -351,7 +365,7 @@
             inner[y, 8:16, :] = low
             inner[y, 144:152, :] = high
 
-    def hand_out(value, keeper, kind, result):
+    def settle(value, keeper, kind, result):
         def put(ref, lead):
             for y in range(2):
                 block = value[y * 128 : (y + 1) * 128, :].T
@@ -366,14 +380,30 @@
         @pl.when(sec != keeper)
         def _():
             put(stage, kind)
-            pltpu.make_async_remote_copy(
-                src_ref=stage.at[kind],
-                dst_ref=result.at[sec],
-                send_sem=out_send.at[kind],
-                recv_sem=out_recv.at[kind],
-                device_id=(other, gy, gz),
-                device_id_type=MESH,
-            ).start()
+
+    two_on = at_depth((depth + 2 + 4 * core) % 8, core)
+    origin = ((depth + 6 - 4 * core) % 8) // 4
+
+    def hand_on(kind):
+        pltpu.make_async_remote_copy(
+            src_ref=stage.at[kind],
+            dst_ref=midway.at[kind],
+            send_sem=out_send.at[kind],
+            recv_sem=mid_recv.at[kind],
+            device_id=two_on,
+            device_id_type=MESH,
+        ).start()
+
+    def hand_over(kind, result):
+        landed(midway.at[kind], mid_recv.at[kind])
+        pltpu.make_async_remote_copy(
+            src_ref=midway.at[kind],
+            dst_ref=result.at[origin],
+            send_sem=mid_send.at[kind],
+            recv_sem=out_recv.at[kind],
+            device_id=two_on,
+            device_id_type=MESH,
+        ).start()
 
     def joined(product):
         cells = product.shape[0] // 2
@@ -405,11 +435,8 @@
         first = 2 * pair
         await_rims(pair)
 
-        def put_wide(rows, cols, value):
-            wide_patch[pair, rows, cols] = value
-
-        fill_wide(pair, put_wide)
-        value = across(wide_patch[pair], first)
+        fill_wide(pair, wide_lines.at[pair], wide_rims.at[pair])
+        value = across(wide_taps(wide_lines.at[pair], wide_rims.at[pair]), first)
         wide_pre[pair] = value
         keep_inner(active(value))
 
@@ -418,11 +445,8 @@
             relay(1, range(EARLY, CHUNKS))
             receive(1)
 
-        def put(rows, cols, value):
-            patch[pair, rows, cols] = value
-
-        fill_inner(put)
-        value = across(patch[pair], first + 1)
+        fill_inner(lines.at[pair])
+        value = across(inner_taps(lines.at[pair]), first + 1)
         pre[pair] = value
         result = active(value)
 
@@ -430,11 +454,11 @@
         def _():
             keep_own(1, result)
             send_rims(1)
-            hand_out(result, 0, 0, out_act)
+            settle(result, 0, 0, out_act)
 
         @pl.when(pair == 1)
         def _():
-            hand_out(result, 1, 0, out_act)
+            settle(result, 1, 0, out_act)
 
         return carry
 
@@ -583,9 +607,6 @@
         part[layer, 864:865, :] = sums + turned(sums)
         reduce_start(layer)
 
-    def put_slope(rows, cols, value):
-        slope_patch[rows, cols] = value
-
     def backward(step, carry):
         pair = 1 - step
         first = 2 * pair
@@ -593,7 +614,7 @@
         slope = slope_of(flow[...], pre[pair])
         keep_own(slot, slope)
         send_rims(slot)
-        weigh(first + 1, slope, patch[pair, 0:256, :], patch[pair, 256:512, :])
+        weigh(first + 1, slope, *[taps_of(lines.at[pair], at, 128, 0, 2) for at in range(2)])
 
         @pl.when(pair == 0)
         def _():
@@ -601,15 +622,26 @@
             reduce_one(3)
 
         await_rims(slot)
-        fill_wide(slot, put_slope)
-        gradient = back_across(slope_patch[...], first + 1)
+
+        @pl.when(pair == 1)
+        def _():
+            hand_on(0)
+
+        @pl.when(pair == 0)
+        def _():
+            hand_over(0, out_act)
+            reduce_half(1)
+            reduce_one(2)
+            reduce_two(3)
+
+        fill_wide(slot, slope_lines, slope_rims)
+        gradient = back_across(wide_taps(slope_lines, slope_rims), first + 1)
         slope = slope_of(gradient, wide_pre[pair])
         keep_inner(slope)
         weigh(
             first,
             slope[128:384, :],
-            wide_patch[pair, 128:384, :],
-            wide_patch[pair, WIDE + 128 : WIDE + 384, :],
+            *[taps_of(wide_lines.at[pair], at, 128, 1, 2) for at in range(2)],
         )
 
         @pl.when(pair == 1)
@@ -618,29 +650,30 @@
 
         @pl.when(pair == 0)
         def _():
-            reduce_half(1)
-            reduce_one(2)
-            reduce_two(3)
-
-        fill_inner(put_slope)
-        gradient = back_across(slope_patch[0:512, :], first)
+            reduce_one(1)
+            reduce_two(2)
+
+        fill_inner(slope_lines)
+        gradient = back_across(inner_taps(slope_lines), first)
         flow[...] = gradient
 
         @pl.when(pair == 1)
         def _():
-            hand_out(gradient, 1, 1, out_grad)
+            settle(gradient, 1, 1, out_grad)
 
         @pl.when(pair == 0)
         def _():
-            hand_out(gradient, 0, 1, out_grad)
+            settle(gradient, 0, 1, out_grad)
 
         return carry
 
     lax.fori_loop(0, 2, backward, 0)
 
+    hand_on(1)
     for round_at in range(7):
-        for layer in reversed(range(LAYERS)):
-            tick = layer + round_at
+        for layer, tick, ready in ((0, round_at, 0), (1, round_at + 2, 0), (2, round_at, 3), (3, round_at, 3)):
+            if round_at < ready:
+                continue
             if tick < 3:
                 everywhere[tick](layer)
             elif tick < 7:
@@ -649,6 +682,9 @@
                 def _():
                     at_home[tick - 3](layer)
 
+        if round_at == 2:
+            hand_over(1, out_grad)
+
     landed(out_act.at[1 - sec], out_recv.at[0])
     landed(out_grad.at[1 - sec], out_recv.at[1])
 
@@ -677,6 +713,7 @@
             landed(chunk_of(2 * other + i, core, chunk), mate_send.at[i, chunk])
     for kind in range(2):
         landed(stage.at[kind], out_send.at[kind])
+        landed(midway.at[kind], mid_send.at[kind])
 
     def drain_sums(layer, carry):
         home = sec == layer // 2
@@ -738,15 +775,18 @@
         vmem((rows, nz), F32),
         vmem((4, 6, 160, 128), F32),
         vmem((4, 160, 128), F32),
-        vmem((2, 2 * WIDE, TAPS * 128), BF16),
-        vmem((2, 512, TAPS * 128), BF16),
-        vmem((2 * WIDE, TAPS * 128), BF16),
+        vmem((2, 2, 3, 768, 128), BF16),
+        vmem((2, 2, 3, 96, 128), BF16),
+        vmem((2, 2, 3, 512, 128), BF16),
+        vmem((2, 3, 768, 128), BF16),
+        vmem((2, 3, 96, 128), BF16),
         vmem((LAYERS, 256, TAPS * 128), BF16),
         vmem((LAYERS, TAPS * 128, 256), BF16),
         vmem((LAYERS, PACK, 128), F32),
         vmem((2, WIDE, 128), F32),
         vmem((2, 256, 128), F32),
         vmem((256, 128), F32),
+        vmem((2, 256, 128), F32),
         vmem((2, 256, 128), F32),
         vmem((LAYERS, GRAD, 128), F32),
         vmem((LAYERS, 512, 128), F32),
@@ -764,6 +804,8 @@
         dma((2, CHUNKS)),
         dma((2, CHUNKS)),
         dma((2, CHUNKS)),
+        dma((2,)),
+        dma((2,)),
         dma((2,)),
         dma((2,)),
         dma((2, LAYERS)),

time: 92.7 us -> 86 us (0.928)
  Pallas kernels: 92 us -> 85.3 us
    pallas_call x1, Pallas kernels: 90 us -> 83.3 us  [per_device(): pl.pallas_call(body, name='encoder_sections', out_shape=(vmem((micro, row...]
where the time goes in v4:
time: 86 us; the launch traced here: 85.9 us
  Pallas kernels  85.3 us (99%)
    pallas_call x1, Pallas kernels, per_device(): pl.pallas_call(body, name='encoder_sections', out_shape=(vmem((micro, row...  83.3 us
    pallas_call x1, Pallas kernels, per_device(): pl.pallas_call(unpack, name='write_results', out_shape=(jax.ShapeDtypeStr...  1.99 us

profile of v4, /device:TPU:1, one launch (start us, length us, event | category | flops | bytes accessed | tf_op | source)
XLA Modules:
  0.0 85.9 jit_solution(17120065713249820027)
XLA Ops:
  0.6 83.3 %encoder_sections.1 = (f32[2,256,128]{2,1,0:T(8,128)S(1)}, f32[2,256,128]{2,1,0:T(8,128)S(1)}, f32[2,1024,128]{2,1,0:T(8,128)S(1)}) custom-call(f32[2,256,128]{2,1,0:T(8,128)} %bitcast.4, f32[2,27,64,64]{3,2,1,0:T(8,128)} %refs_1_.1, f32[2,64]{1,0:T(2,128)} %refs_2_.1, f32[2,256,128]{2,1,0:T(8,128)} %bitcast.5), custom_call_target="tpu_custom_call" | custom-call | tf_op jit(solution)/shard_map/encoder_sections/pallas_call | solution.py:824
  83.9 2.0 %write_results.1 = (f32[2,256,128]{2,1,0:T(8,128)}, f32[2,256,128]{2,1,0:T(8,128)}, f32[2,27,64,64]{3,2,1,0:T(8,128)}, f32[2,64]{1,0:T(2,128)}) custom-call(f32[2,256,128]{2,1,0:T(8,128)S(1)} %get-tuple-element.11.act, f32[2,256,128]{2,1,0:T(8,128)S(1)} %get-tuple-element.12.grad, f32[2,1024,128]{2,1,0:T(8,128)S(1)} %get-tuple-element.13.total), custom_call_target="tpu_custom_call" | custom-call | tf_op jit(solution)/shard_map/write_results/pallas_call | solution.py:844

commit v5 on v4

--- a/solution.py
+++ b/solution.py
@@ -18,7 +18,8 @@
 CHUNKS = 5
 CHUNK = PACK // 2 // CHUNKS
 EARLY = 3
-GRAD = 1024
+GRAD = 512
+FRONT = 5
 WIDE = 576
 
 
@@ -285,7 +286,8 @@
     for y in range(2):
         flow[y * 128 : (y + 1) * 128, :] = turned_in(cotangent, y)
     for layer in range(LAYERS):
-        part[layer, 864:GRAD, :] = jnp.zeros((GRAD - 864, 128), F32)
+        for half, used in ((0, FRONT * TAP_ROWS), (1, (TAPS - FRONT) * TAP_ROWS)):
+            part[2 * layer + half, used:GRAD, :] = jnp.zeros((GRAD - used, 128), F32)
 
     def relay(i, chunks):
         for chunk in chunks:
@@ -343,14 +345,15 @@
         )
 
     def wide_taps(line_ref, edge_ref):
-        blocks = []
-        for at in range(2):
-            blocks.append(taps_of(line_ref, at, 128, 0, 4))
-            blocks.append(taps_of(edge_ref, at, 16, 0, 4))
-        return jnp.concatenate(blocks, axis=0)
+        return [
+            jnp.concatenate(
+                [taps_of(line_ref, at, 128, 0, 4), taps_of(edge_ref, at, 16, 0, 4)], axis=0
+            )
+            for at in range(2)
+        ]
 
     def inner_taps(line_ref):
-        return jnp.concatenate([taps_of(line_ref, at, 128, 0, 2) for at in range(2)], axis=0)
+        return [taps_of(line_ref, at, 128, 0, 2) for at in range(2)]
 
     def keep_inner(value):
         for y in range(4):
@@ -405,20 +408,23 @@
             device_id_type=MESH,
         ).start()
 
-    def joined(product):
-        cells = product.shape[0] // 2
-        return (product[:cells, 0:128] + product[:cells, 128:256]) + (
-            product[cells:, 0:128] + product[cells:, 128:256]
-        )
-
-    def across(patches, layer):
-        product = lax.dot_general(
-            patches, wide_f[layer], (((1,), (1,)), ((), ())), preferred_element_type=F32
-        )
-        return joined(product) + packed[layer, 864:865, :]
-
-    def back_across(patches, layer):
-        return joined(jnp.dot(patches, wide_b[layer], preferred_element_type=F32))
+    def joined(parts, columns, dims):
+        high, low = parts
+        both = lax.dot_general(high, columns(256), dims, preferred_element_type=F32)
+        rest = lax.dot_general(low, columns(128), dims, preferred_element_type=F32)
+        return both[:, 0:128] + (both[:, 128:256] + rest)
+
+    def across(parts, layer):
+        def columns(count):
+            return wide_f[layer, 0:count, :]
+
+        return joined(parts, columns, (((1,), (1,)), ((), ()))) + packed[layer, 864:865, :]
+
+    def back_across(parts, layer):
+        def columns(count):
+            return wide_b[layer, :, 0:count]
+
+        return joined(parts, columns, (((1,), (0,)), ((), ())))
 
     def active(value):
         return value * (1.0 / (1.0 + jnp.exp(-value)))
@@ -466,9 +472,9 @@
 
     index_one = px + core * (gz - px)
     index_two = gz + core * (px - gz)
-    offset_half = core * 512
-    offset_one = offset_half + index_one * 128
-    offset_two = offset_one + index_two * 32
+    offset_half = core * 256
+    offset_one = offset_half + index_one * 64
+    offset_two = offset_one + index_two * 16
 
     def rows_at(ref, layer, start, size):
         return ref.at[layer, pl.ds(pl.multiple_of(start, 8), size), :]
@@ -485,7 +491,7 @@
 
     def reduce_start(layer):
         push(
-            rows_at(part, layer, (1 - core) * 512, 512),
+            rows_at(part, layer, (1 - core) * 256, 256),
             half_in.at[layer],
             pair_send.at[0, layer],
             pair_recv.at[0, layer],
@@ -495,12 +501,12 @@
     def reduce_half(layer):
         landed(half_in.at[layer], pair_recv.at[0, layer])
         half_sum[layer] = (
-            part[layer, pl.ds(pl.multiple_of(offset_half, 8), 512), :] + half_in[layer]
+            part[layer, pl.ds(pl.multiple_of(offset_half, 8), 256), :] + half_in[layer]
         )
         for d in range(1, 4):
             peer = (index_one + d) % 4
             push(
-                rows_at(half_sum, layer, peer * 128, 128),
+                rows_at(half_sum, layer, peer * 64, 64),
                 one_in.at[layer, 3 - d],
                 group_send.at[0, layer, 3 - d],
                 group_recv.at[0, layer, 3 - d],
@@ -510,12 +516,12 @@
     def reduce_one(layer):
         for s in range(3):
             landed(one_in.at[layer, s], group_recv.at[0, layer, s])
-        own = half_sum[layer, pl.ds(pl.multiple_of(index_one * 128, 8), 128), :]
+        own = half_sum[layer, pl.ds(pl.multiple_of(index_one * 64, 8), 64), :]
         one_sum[layer] = (own + one_in[layer, 0]) + (one_in[layer, 1] + one_in[layer, 2])
         for d in range(1, 4):
             peer = (index_two + d) % 4
             push(
-                rows_at(one_sum, layer, peer * 32, 32),
+                rows_at(one_sum, layer, peer * 16, 16),
                 two_in.at[layer, 3 - d],
                 group_send.at[1, layer, 3 - d],
                 group_recv.at[1, layer, 3 - d],
@@ -525,12 +531,12 @@
     def reduce_two(layer):
         for s in range(3):
             landed(two_in.at[layer, s], group_recv.at[1, layer, s])
-        own = one_sum[layer, pl.ds(pl.multiple_of(index_two * 32, 8), 32), :]
+        own = one_sum[layer, pl.ds(pl.multiple_of(index_two * 16, 8), 16), :]
         two_sum[layer] = (own + two_in[layer, 0]) + (two_in[layer, 1] + two_in[layer, 2])
         for d in range(1, 8):
             peer = (depth + d) % 8
 
-            @pl.when(peer // 4 == layer // 2)
+            @pl.when(peer // 4 == layer // 4)
             def _():
                 push(
                     two_sum.at[layer],
@@ -543,7 +549,7 @@
     def gathered(layer, stage_at, base, index, size):
         for s in range(3):
             sender = (index + 1 + s) % 4
-            piece = rows_at(final, layer % 2, base + sender * size, size)
+            piece = rows_at(final, layer % 4, base + sender * size, size)
             landed(piece, group_recv.at[stage_at, layer, s])
 
     def gather_two(layer):
@@ -553,9 +559,9 @@
         total = three_in[layer, 0]
         for level in range(1, 8):
             total = total + three_in[layer, level]
-        final[layer % 2, pl.ds(pl.multiple_of(offset_two, 8), 32), :] = total * scale
+        final[layer % 4, pl.ds(pl.multiple_of(offset_two, 8), 16), :] = total * scale
         for d in range(1, 4):
-            piece = rows_at(final, layer % 2, offset_two, 32)
+            piece = rows_at(final, layer % 4, offset_two, 16)
             push(
                 piece,
                 piece,
@@ -565,9 +571,9 @@
             )
 
     def gather_one(layer):
-        gathered(layer, 2, offset_one, index_two, 32)
+        gathered(layer, 2, offset_one, index_two, 16)
         for d in range(1, 4):
-            piece = rows_at(final, layer % 2, offset_one, 128)
+            piece = rows_at(final, layer % 4, offset_one, 64)
             push(
                 piece,
                 piece,
@@ -577,12 +583,12 @@
             )
 
     def gather_half(layer):
-        gathered(layer, 3, offset_half, index_one, 128)
-        piece = rows_at(final, layer % 2, offset_half, 512)
+        gathered(layer, 3, offset_half, index_one, 64)
+        piece = rows_at(final, layer % 4, offset_half, 256)
         push(piece, piece, pair_send.at[1, layer], pair_recv.at[1, layer], mate)
 
     def finish(layer):
-        piece = rows_at(final, layer % 2, (1 - core) * 512, 512)
+        piece = rows_at(final, layer % 4, (1 - core) * 256, 256)
         landed(piece, pair_recv.at[1, layer])
 
     everywhere = [reduce_half, reduce_one, reduce_two]
@@ -594,18 +600,21 @@
         product = jnp.dot(sides, high_patch, preferred_element_type=F32) + jnp.dot(
             sides, low_patch, preferred_element_type=F32
         )
+        sums = jnp.sum(slope, axis=0, keepdims=True)
+        part[2 * layer, FRONT * TAP_ROWS : FRONT * TAP_ROWS + 1, :] = sums + turned(sums)
         for tap in range(TAPS):
             cols = slice(tap * 128, tap * 128 + 128)
             block = product[0:128, cols] + product[128:256, cols]
-            base = tap * TAP_ROWS
+            at = 2 * layer + tap // FRONT
+            base = tap % FRONT * TAP_ROWS
             flipped = turned(block[64:128, :])
-            part[layer, base : base + 64, :] = block[0:64, :] + jnp.where(left, flipped, 0.0)
-            part[layer, base + 64 : base + 96, :] = jnp.where(
+            part[at, base : base + 64, :] = block[0:64, :] + jnp.where(left, flipped, 0.0)
+            part[at, base + 64 : base + 96, :] = jnp.where(
                 left, block[64:96, :], flipped[32:64, :]
             )
-        sums = jnp.sum(slope, axis=0, keepdims=True)
-        part[layer, 864:865, :] = sums + turned(sums)
-        reduce_start(layer)
+            if tap == FRONT - 1:
+                reduce_start(2 * layer)
+        reduce_start(2 * layer + 1)
 
     def backward(step, carry):
         pair = 1 - step
@@ -618,8 +627,9 @@
 
         @pl.when(pair == 0)
         def _():
-            reduce_half(2)
-            reduce_one(3)
+            for half in range(2):
+                reduce_half(4 + half)
+                reduce_one(6 + half)
 
         await_rims(slot)
 
@@ -630,9 +640,10 @@
         @pl.when(pair == 0)
         def _():
             hand_over(0, out_act)
-            reduce_half(1)
-            reduce_one(2)
-            reduce_two(3)
+            for half in range(2):
+                reduce_half(2 + half)
+                reduce_one(4 + half)
+                reduce_two(6 + half)
 
         fill_wide(slot, slope_lines, slope_rims)
         gradient = back_across(wide_taps(slope_lines, slope_rims), first + 1)
@@ -646,12 +657,14 @@
 
         @pl.when(pair == 1)
         def _():
-            reduce_half(3)
+            for half in range(2):
+                reduce_half(6 + half)
 
         @pl.when(pair == 0)
         def _():
-            reduce_one(1)
-            reduce_two(2)
+            for half in range(2):
+                reduce_one(2 + half)
+                reduce_two(4 + half)
 
         fill_inner(slope_lines)
         gradient = back_across(inner_taps(slope_lines), first)
@@ -671,16 +684,17 @@
 
     hand_on(1)
     for round_at in range(7):
-        for layer, tick, ready in ((0, round_at, 0), (1, round_at + 2, 0), (2, round_at, 3), (3, round_at, 3)):
-            if round_at < ready:
+        for at in range(2 * LAYERS):
+            tick = round_at + (2 if at in (2, 3) else 0)
+            if at >= 4 and round_at < 3:
                 continue
             if tick < 3:
-                everywhere[tick](layer)
+                everywhere[tick](at)
             elif tick < 7:
 
-                @pl.when(sec == layer // 2)
+                @pl.when(sec == at // 4)
                 def _():
-                    at_home[tick - 3](layer)
+                    at_home[tick - 3](at)
 
         if round_at == 2:
             hand_over(1, out_grad)
@@ -716,14 +730,14 @@
         landed(midway.at[kind], mid_send.at[kind])
 
     def drain_sums(layer, carry):
-        home = sec == layer // 2
+        home = sec == layer // 4
         landed(half_in.at[layer], pair_send.at[0, layer])
         for s in range(3):
             landed(one_in.at[layer, s], group_send.at[0, layer, s])
             landed(two_in.at[layer, s], group_send.at[1, layer, s])
         for d in range(1, 8):
 
-            @pl.when(((depth + d) % 8) // 4 == layer // 2)
+            @pl.when(((depth + d) % 8) // 4 == layer // 4)
             def _():
                 landed(two_sum.at[layer], deep_send.at[layer, d - 1])
 
@@ -736,7 +750,7 @@
 
         return carry
 
-    lax.fori_loop(0, LAYERS, drain_sums, 0)
+    lax.fori_loop(0, 2 * LAYERS, drain_sums, 0)
 
 
 def unpack(act, grad, total, out_act, out_grad, out_weight, out_bias, spread, sem):
@@ -748,16 +762,18 @@
         copy.start()
     for i in range(2):
         for tap in range(TAPS):
-            base = tap * TAP_ROWS
-            top = total[i, base : base + 64, :]
-            near = total[i, base + 64 : base + 96, :]
+            at = 2 * i + tap // FRONT
+            base = tap % FRONT * TAP_ROWS
+            top = total[at, base : base + 64, :]
+            near = total[at, base + 64 : base + 96, :]
             spread[i, 9 + tap] = top[:, 0:64]
             spread[i, 18 + tap] = pltpu.roll(top, 64, 1)[:, 0:64]
             spread[i, tap, 0:32, :] = near[:, 0:64]
             spread[i, tap, 32:64, :] = pltpu.roll(near, 64, 1)[:, 0:64]
         copies.append(pltpu.make_async_copy(spread.at[i], out_weight.at[i], sem.at[2 + i]))
         copies[-1].start()
-    out_bias[...] = total[:, 864, 0:64]
+        row = FRONT * TAP_ROWS
+        out_bias[i : i + 1, :] = total[2 * i, row : row + 1, 0:64]
     for copy in copies:
         copy.wait()
 
@@ -788,14 +804,14 @@
         vmem((256, 128), F32),
         vmem((2, 256, 128), F32),
         vmem((2, 256, 128), F32),
-        vmem((LAYERS, GRAD, 128), F32),
-        vmem((LAYERS, 512, 128), F32),
-        vmem((LAYERS, 512, 128), F32),
-        vmem((LAYERS, 3, 128, 128), F32),
-        vmem((LAYERS, 128, 128), F32),
-        vmem((LAYERS, 3, 32, 128), F32),
-        vmem((LAYERS, 32, 128), F32),
-        vmem((LAYERS, 8, 32, 128), F32),
+        vmem((2 * LAYERS, GRAD, 128), F32),
+        vmem((2 * LAYERS, 256, 128), F32),
+        vmem((2 * LAYERS, 256, 128), F32),
+        vmem((2 * LAYERS, 3, 64, 128), F32),
+        vmem((2 * LAYERS, 64, 128), F32),
+        vmem((2 * LAYERS, 3, 16, 128), F32),
+        vmem((2 * LAYERS, 16, 128), F32),
+        vmem((2 * LAYERS, 8, 16, 128), F32),
         dma((3,)),
         dma((4, 8)),
         dma((4, 8)),
@@ -808,12 +824,12 @@
         dma((2,)),
         dma((2,)),
         dma((2,)),
-        dma((2, LAYERS)),
-        dma((2, LAYERS)),
-        dma((4, LAYERS, 3)),
-        dma((4, LAYERS, 3)),
-        dma((LAYERS, 7)),
-        dma((LAYERS, 7)),
+        dma((2, 2 * LAYERS)),
+        dma((2, 2 * LAYERS)),
+        dma((4, 2 * LAYERS, 3)),
+        dma((4, 2 * LAYERS, 3)),
+        dma((2 * LAYERS, 7)),
+        dma((2 * LAYERS, 7)),
     ]
     near = pl.BlockSpec(memory_space=pltpu.VMEM)
     far = pl.BlockSpec(memory_space=pl.ANY)
@@ -827,7 +843,7 @@
         out_shape=(
             vmem((micro, rows, nz), F32),
             vmem((micro, rows, nz), F32),
-            vmem((2, GRAD, 128), F32),
+            vmem((4, GRAD, 128), F32),
         ),
         in_specs=[far, far, near, far],
         out_specs=(near,) * 3,

time: 86 us -> 85.8 us (level)
  no operation moved by 1% of the time
where the time goes in v5:
time: 85.8 us; the launch traced here: 85.7 us
  Pallas kernels  85.1 us (99%)
    pallas_call x1, Pallas kernels, per_device(): pl.pallas_call(body, name='encoder_sections', out_shape=(vmem((micro, row...  83.1 us
    pallas_call x1, Pallas kernels, per_device(): pl.pallas_call(unpack, name='write_results', out_shape=(jax.ShapeDtypeStr...  1.99 us

profile of v5, /device:TPU:1, one launch (start us, length us, event | category | flops | bytes accessed | tf_op | source)
XLA Modules:
  0.0 85.7 jit_solution(18154133876908651574)
XLA Ops:
  0.6 83.1 %encoder_sections.1 = (f32[2,256,128]{2,1,0:T(8,128)S(1)}, f32[2,256,128]{2,1,0:T(8,128)S(1)}, f32[4,512,128]{2,1,0:T(8,128)S(1)}) custom-call(f32[2,256,128]{2,1,0:T(8,128)} %bitcast.4, f32[2,27,64,64]{3,2,1,0:T(8,128)} %refs_1_.1, f32[2,64]{1,0:T(2,128)} %refs_2_.1, f32[2,256,128]{2,1,0:T(8,128)} %bitcast.5), custom_call_target="tpu_custom_call" | custom-call | tf_op jit(solution)/shard_map/encoder_sections/pallas_call | solution.py:840
  83.7 2.0 %write_results.1 = (f32[2,256,128]{2,1,0:T(8,128)}, f32[2,256,128]{2,1,0:T(8,128)}, f32[2,27,64,64]{3,2,1,0:T(8,128)}, f32[2,64]{1,0:T(2,128)}) custom-call(f32[2,256,128]{2,1,0:T(8,128)S(1)} %get-tuple-element.11.act, f32[2,256,128]{2,1,0:T(8,128)S(1)} %get-tuple-element.12.grad, f32[4,512,128]{2,1,0:T(8,128)S(1)} %get-tuple-element.13.total), custom_call_target="tpu_custom_call" | custom-call | tf_op jit(solution)/shard_map/write_results/pallas_call | solution.py:860

commit v6 on v5

--- a/solution.py
+++ b/solution.py
@@ -612,9 +612,10 @@
             part[at, base + 64 : base + 96, :] = jnp.where(
                 left, block[64:96, :], flipped[32:64, :]
             )
-            if tap == FRONT - 1:
-                reduce_start(2 * layer)
-        reduce_start(2 * layer + 1)
+
+    def both(stage_of, layer):
+        stage_of(2 * layer)
+        stage_of(2 * layer + 1)
 
     def backward(step, carry):
         pair = 1 - step
@@ -624,26 +625,21 @@
         keep_own(slot, slope)
         send_rims(slot)
         weigh(first + 1, slope, *[taps_of(lines.at[pair], at, 128, 0, 2) for at in range(2)])
+        reduce_start(2 * first + 2)
+        reduce_start(2 * first + 3)
+        await_rims(slot)
+
+        @pl.when(pair == 1)
+        def _():
+            hand_on(0)
+            both(reduce_half, 3)
 
         @pl.when(pair == 0)
         def _():
-            for half in range(2):
-                reduce_half(4 + half)
-                reduce_one(6 + half)
-
-        await_rims(slot)
-
-        @pl.when(pair == 1)
-        def _():
-            hand_on(0)
-
-        @pl.when(pair == 0)
-        def _():
             hand_over(0, out_act)
-            for half in range(2):
-                reduce_half(2 + half)
-                reduce_one(4 + half)
-                reduce_two(6 + half)
+            both(reduce_start, 2)
+            both(reduce_one, 3)
+            both(reduce_half, 1)
 
         fill_wide(slot, slope_lines, slope_rims)
         gradient = back_across(wide_taps(slope_lines, slope_rims), first + 1)
@@ -655,16 +651,12 @@
             *[taps_of(wide_lines.at[pair], at, 128, 1, 2) for at in range(2)],
         )
 
-        @pl.when(pair == 1)
-        def _():
-            for half in range(2):
-                reduce_half(6 + half)
-
         @pl.when(pair == 0)
         def _():
-            for half in range(2):
-                reduce_one(2 + half)
-                reduce_two(4 + half)
+            both(reduce_start, 0)
+            both(reduce_two, 3)
+            both(reduce_one, 1)
+            both(reduce_half, 2)
 
         fill_inner(slope_lines)
         gradient = back_across(inner_taps(slope_lines), first)
@@ -683,18 +675,19 @@
     lax.fori_loop(0, 2, backward, 0)
 
     hand_on(1)
+    ahead = {0: 0, 1: 2, 2: 1, 3: 3}
     for round_at in range(7):
-        for at in range(2 * LAYERS):
-            tick = round_at + (2 if at in (2, 3) else 0)
-            if at >= 4 and round_at < 3:
-                continue
+        for layer in range(LAYERS):
+            tick = round_at + ahead[layer]
+            if layer >= 2 and tick >= 3:
+                tick = round_at if round_at >= 3 else 7
             if tick < 3:
-                everywhere[tick](at)
+                both(everywhere[tick], layer)
             elif tick < 7:
 
-                @pl.when(sec == at // 4)
+                @pl.when(sec == layer // 2)
                 def _():
-                    at_home[tick - 3](at)
+                    both(at_home[tick - 3], layer)
 
         if round_at == 2:
             hand_over(1, out_grad)

time: 85.8 us -> 86.6 us (level)
  no operation moved by 1% of the time
where the time goes in v6:
time: 86.6 us; the launch traced here: 86.5 us
  Pallas kernels  85.9 us (99%)
    pallas_call x1, Pallas kernels, per_device(): pl.pallas_call(body, name='encoder_sections', out_shape=(vmem((micro, row...  83.9 us
    pallas_call x1, Pallas kernels, per_device(): pl.pallas_call(unpack, name='write_results', out_shape=(jax.ShapeDtypeStr...  1.99 us

profile of v6, /device:TPU:1, one launch (start us, length us, event | category | flops | bytes accessed | tf_op | source)
XLA Modules:
  0.0 86.5 jit_solution(9963200394513151008)
XLA Ops:
  0.6 83.9 %encoder_sections.1 = (f32[2,256,128]{2,1,0:T(8,128)S(1)}, f32[2,256,128]{2,1,0:T(8,128)S(1)}, f32[4,512,128]{2,1,0:T(8,128)S(1)}) custom-call(f32[2,256,128]{2,1,0:T(8,128)} %bitcast.4, f32[2,27,64,64]{3,2,1,0:T(8,128)} %refs_1_.1, f32[2,64]{1,0:T(2,128)} %refs_2_.1, f32[2,256,128]{2,1,0:T(8,128)} %bitcast.5), custom_call_target="tpu_custom_call" | custom-call | tf_op jit(solution)/shard_map/encoder_sections/pallas_call | solution.py:833
  84.5 2.0 %write_results.1 = (f32[2,256,128]{2,1,0:T(8,128)}, f32[2,256,128]{2,1,0:T(8,128)}, f32[2,27,64,64]{3,2,1,0:T(8,128)}, f32[2,64]{1,0:T(2,128)}) custom-call(f32[2,256,128]{2,1,0:T(8,128)S(1)} %get-tuple-element.11.act, f32[2,256,128]{2,1,0:T(8,128)S(1)} %get-tuple-element.12.grad, f32[4,512,128]{2,1,0:T(8,128)S(1)} %get-tuple-element.13.total), custom_call_target="tpu_custom_call" | custom-call | tf_op jit(solution)/shard_map/write_results/pallas_call | solution.py:853

commit v7 on v4

--- a/solution.py
+++ b/solution.py
@@ -15,9 +15,9 @@
 DIRS = [(dy, dz) for dy in (-1, 0, 1) for dz in (-1, 0, 1) if (dy, dz) != (0, 0)]
 TAP_ROWS = 96
 PACK = 880
-CHUNKS = 5
+CHUNKS = 11
 CHUNK = PACK // 2 // CHUNKS
-EARLY = 3
+EARLY = 6
 GRAD = 1024
 WIDE = 576
 
@@ -343,14 +343,15 @@
         )
 
     def wide_taps(line_ref, edge_ref):
-        blocks = []
-        for at in range(2):
-            blocks.append(taps_of(line_ref, at, 128, 0, 4))
-            blocks.append(taps_of(edge_ref, at, 16, 0, 4))
-        return jnp.concatenate(blocks, axis=0)
+        return [
+            jnp.concatenate(
+                [taps_of(line_ref, at, 128, 0, 4), taps_of(edge_ref, at, 16, 0, 4)], axis=0
+            )
+            for at in range(2)
+        ]
 
     def inner_taps(line_ref):
-        return jnp.concatenate([taps_of(line_ref, at, 128, 0, 2) for at in range(2)], axis=0)
+        return [taps_of(line_ref, at, 128, 0, 2) for at in range(2)]
 
     def keep_inner(value):
         for y in range(4):
@@ -405,20 +406,23 @@
             device_id_type=MESH,
         ).start()
 
-    def joined(product):
-        cells = product.shape[0] // 2
-        return (product[:cells, 0:128] + product[:cells, 128:256]) + (
-            product[cells:, 0:128] + product[cells:, 128:256]
-        )
-
-    def across(patches, layer):
-        product = lax.dot_general(
-            patches, wide_f[layer], (((1,), (1,)), ((), ())), preferred_element_type=F32
-        )
-        return joined(product) + packed[layer, 864:865, :]
-
-    def back_across(patches, layer):
-        return joined(jnp.dot(patches, wide_b[layer], preferred_element_type=F32))
+    def joined(parts, columns, dims):
+        high, low = parts
+        both = lax.dot_general(high, columns(256), dims, preferred_element_type=F32)
+        rest = lax.dot_general(low, columns(128), dims, preferred_element_type=F32)
+        return both[:, 0:128] + (both[:, 128:256] + rest)
+
+    def across(parts, layer):
+        def columns(count):
+            return wide_f[layer, 0:count, :]
+
+        return joined(parts, columns, (((1,), (1,)), ((), ()))) + packed[layer, 864:865, :]
+
+    def back_across(parts, layer):
+        def columns(count):
+            return wide_b[layer, :, 0:count]
+
+        return joined(parts, columns, (((1,), (0,)), ((), ())))
 
     def active(value):
         return value * (1.0 / (1.0 + jnp.exp(-value)))

time: 86 us -> 83.6 us (0.972)
  Pallas kernels: 85.3 us -> 82.8 us
    pallas_call x1, Pallas kernels: 83.3 us -> 80.8 us  [per_device(): pl.pallas_call(body, name='encoder_sections', out_shape=(vmem((micro, row...]
where the time goes in v7:
time: 83.6 us; the launch traced here: 83.4 us
  Pallas kernels  82.8 us (99%)
    pallas_call x1, Pallas kernels, per_device(): pl.pallas_call(body, name='encoder_sections', out_shape=(vmem((micro, row...  80.8 us
    pallas_call x1, Pallas kernels, per_device(): pl.pallas_call(unpack, name='write_results', out_shape=(jax.ShapeDtypeStr...  1.99 us

profile of v7, /device:TPU:1, one launch (start us, length us, event | category | flops | bytes accessed | tf_op | source)
XLA Modules:
  0.0 83.4 jit_solution(12863874421201633859)
XLA Ops:
  0.6 80.8 %encoder_sections.1 = (f32[2,256,128]{2,1,0:T(8,128)S(1)}, f32[2,256,128]{2,1,0:T(8,128)S(1)}, f32[2,1024,128]{2,1,0:T(8,128)S(1)}) custom-call(f32[2,256,128]{2,1,0:T(8,128)} %bitcast.4, f32[2,27,64,64]{3,2,1,0:T(8,128)} %refs_1_.1, f32[2,64]{1,0:T(2,128)} %refs_2_.1, f32[2,256,128]{2,1,0:T(8,128)} %bitcast.5), custom_call_target="tpu_custom_call" | custom-call | tf_op jit(solution)/shard_map/encoder_sections/pallas_call | solution.py:828
  81.4 2.0 %write_results.1 = (f32[2,256,128]{2,1,0:T(8,128)}, f32[2,256,128]{2,1,0:T(8,128)}, f32[2,27,64,64]{3,2,1,0:T(8,128)}, f32[2,64]{1,0:T(2,128)}) custom-call(f32[2,256,128]{2,1,0:T(8,128)S(1)} %get-tuple-element.11.act, f32[2,256,128]{2,1,0:T(8,128)S(1)} %get-tuple-element.12.grad, f32[2,1024,128]{2,1,0:T(8,128)S(1)} %get-tuple-element.13.total), custom_call_target="tpu_custom_call" | custom-call | tf_op jit(solution)/shard_map/write_results/pallas_call | solution.py:848
